TPU v7x, 512 devices: a whole 4x8x8 slice. The times are simulated.
512 devices in a mesh: dp: 32 (over x, y), table: 16 (over z, core).
Axes of the slice: x: 4, y: 8, z: 8, core: 2. Of those that a mesh axis runs over, the one named last changes fastest.
Arguments:
- table: bfloat16 [12288, 512], P('table'), may hold values from -6 to 6
- history_shard: int32 [512, 256, 1], P(('dp', 'table')), may hold values from 0 to 15; in each aligned block of 256 rows (0 to 255, 256 to 511, ..., all dimensions but the last counted through in order) at most 32 rows name the same one
- history_row: int32 [512, 256], P(('dp', 'table')), may hold values from 0 to 767
- lengths: int32 [512], P(('dp', 'table')), may hold values from 1 to 256, 98304 in all
- w_in: bfloat16 [512, 2048], replicated, may hold values from -0.25 to 0.25
- w_out: bfloat16 [512, 512], replicated, may hold values from -0.25 to 0.25
- cotangent: bfloat16 [512, 256, 512], P(('dp', 'table')), may hold values from -6 to 6
Outputs:
- table_grad: float32 [12288, 512], P('table')
- dense_grad: bfloat16 [512, 512], replicated
Inputs may be any that keep to these rules, and one draw needn't show every extreme that they name: `history_shard`: among the 256 history slots of one device's samples, at most 32 name one table shard, and that bound is met by some shard in some device's slots. `lengths`: some sample has the full length 256.
All inputs are finite; a program needn't handle non-finite values. No bound on the sum of `lengths` on one device may be relied on, other than what follows from the above.
Results may differ from a plain program's by a relative error of at most 0.017.
Values may be sent and summed in bfloat16 or wider, within the bound.
A program may use at most 64 MiB of HBM per device.

v0:
```python
import math

import jax
import jax.numpy as jnp
from jax import lax
from jax.sharding import PartitionSpec as P

HEADS = 4


def layer_norm(values):
    average = jnp.mean(values, axis=-1, keepdims=True)
    centred = values - average
    variance = jnp.mean(centred * centred, axis=-1, keepdims=True)
    return centred * lax.rsqrt(variance + 1e-06)


def hstu_layer(embedded, w_in, w_out, lengths):
    samples_here, seq_span, model_width = embedded.shape
    head_dim = model_width // HEADS
    normed = layer_norm(embedded.astype(jnp.float32)).astype(jnp.bfloat16)
    projected = jax.nn.silu(
        jnp.dot(
            normed.reshape(samples_here * seq_span, model_width),
            w_in,
            preferred_element_type=jnp.float32,
        )
    )
    gate_part = projected[:, :model_width]
    shaped = (samples_here, seq_span, HEADS, head_dim)
    values = projected[:, model_width : 2 * model_width].astype(jnp.bfloat16).reshape(shaped)
    queries = projected[:, 2 * model_width : 3 * model_width].astype(jnp.bfloat16).reshape(shaped)
    keys = projected[:, 3 * model_width :].astype(jnp.bfloat16).reshape(shaped)
    scores = jnp.einsum(
        "blhd,bmhd->bhlm", queries.astype(jnp.float32), keys.astype(jnp.float32)
    ) * head_dim ** (-0.5)
    positions = jnp.arange(seq_span)
    live_keys = (positions[None, None, :] <= positions[None, :, None]) & (
        positions[None, None, :] < lengths[:, None, None]
    )
    weights = (
        jnp.where(live_keys[:, None], jax.nn.silu(scores), 0.0)
        / lengths.astype(jnp.float32)[:, None, None, None]
    )
    weights = weights.astype(jnp.bfloat16)
    attended = jnp.einsum(
        "bhlm,bmhd->blhd", weights.astype(jnp.float32), values.astype(jnp.float32)
    ).reshape(samples_here * seq_span, model_width)
    mixed = (layer_norm(attended) * gate_part).astype(jnp.bfloat16)
    output = jnp.dot(mixed, w_out, preferred_element_type=jnp.float32) + embedded.reshape(
        -1, model_width
    ).astype(jnp.float32)
    return (output, mixed)


def per_device(table, history_shard, history_row, lengths, w_in, w_out, cotangent):
    shard_rows, model_width = table.shape
    samples_here, seq_span = history_row.shape
    groups = lax.axis_size("table")
    slot_count = samples_here * seq_span
    capacity = 2 * slot_count // groups
    owners = history_shard[:, :, 0].reshape(-1)
    local_rows = history_row.reshape(-1)
    owner_hits = (owners[:, None] == jnp.arange(groups)[None, :]).astype(jnp.int32)
    slot_rank = jnp.sum((jnp.cumsum(owner_hits, axis=0) - owner_hits) * owner_hits, axis=1)
    position = owners * capacity + slot_rank
    requested = (
        jnp.zeros((groups * capacity,), jnp.int32)
        .at[position]
        .set(local_rows)
        .reshape(groups, capacity)
    )
    incoming = lax.all_to_all(requested, "table", split_axis=0, concat_axis=0, tiled=True).reshape(
        -1
    )
    global_rows = owners * shard_rows + local_rows
    piece = lax.all_gather(table, "table", axis=0, tiled=True)
    inside = (global_rows >= 0) & (global_rows < piece.shape[0])
    taken = piece[jnp.clip(global_rows, 0, piece.shape[0] - 1)].astype(jnp.float32)
    embedded = jnp.where(inside[:, None], taken, 0.0).astype(jnp.bfloat16)
    embedded = embedded.reshape(samples_here, seq_span, model_width)
    output, pullback, mixed = jax.vjp(
        lambda rows_in: hstu_layer(rows_in, w_in, w_out, lengths), embedded, has_aux=True
    )
    row_live = jnp.arange(seq_span)[None, :] < lengths[:, None]
    grad_seed = jnp.where(row_live[:, :, None], cotangent, jnp.zeros_like(cotangent))
    flat_seed = grad_seed.reshape(-1, model_width)
    (row_grad,) = pullback(flat_seed.astype(jnp.float32))
    dense_part = jnp.dot(mixed.T, flat_seed, preferred_element_type=jnp.float32)
    outgoing = (
        jnp.zeros((groups * capacity, model_width), jnp.bfloat16)
        .at[position]
        .set(row_grad.reshape(-1, model_width))
    )
    arrived = lax.all_to_all(
        outgoing.reshape(groups, capacity, model_width),
        "table",
        split_axis=0,
        concat_axis=0,
        tiled=True,
    )
    local_grad = (
        jnp.zeros((shard_rows, model_width), jnp.float32)
        .at[incoming]
        .add(arrived.reshape(-1, model_width).astype(jnp.float32))
    )
    total_slots = slot_count * lax.axis_size("dp") * groups
    grad_scale = 1.0 / math.sqrt(total_slots)
    table_grad = lax.psum(local_grad, "dp")
    dense_total = lax.psum(dense_part, ("dp", "table"))
    dense_grad = (dense_total * grad_scale).astype(jnp.bfloat16)
    return (table_grad, dense_grad)


def solution(mesh):
    in_specs = (
        P("table", None),
        P(("dp", "table"), None, None),
        P(("dp", "table"), None),
        P(("dp", "table")),
        P(),
        P(),
        P(("dp", "table"), None, None),
    )
    out_specs = (P("table", None), P())
    return jax.shard_map(
        per_device, mesh=mesh, in_specs=in_specs, out_specs=out_specs, check_vma=False
    )
```

profile of v0, /device:TPU:1, one launch (start us, length us, event | category | flops | bytes accessed | tf_op | source)
XLA Modules:
  0.0 580.3 jit_solution(10138484838293075610)
XLA Ops:
  7.2 0.7 all-gather.2.cloned.1.call-update
  7.9 0.7 fusion.64
  8.6 0.6 reduce-window.6
  9.2 0.2 slice_reduce_fusion
  9.4 0.8 fusion.63
  10.2 0.7 compare_select_fusion.1
  10.9 1.6 scatter_custom_fusion
  12.4 0.7 all_to_all.9
  13.1 11.8 %all-to-all-start = ((s32[16,1,32]{2,1,0:T(1,128)}), s32[16,1,32]{2,1,0:T(1,128)S(1)}, u32[]{:S(2)}, u32[]{:S(2)}) async-start(s32[16,1,32]{2,1,0:T(1,128)} %all_to_all.9), calls=%async_computation | async-start | bytes 16384 | tf_op jit(solution)/shard_map/all_to_all | solution.py:73
  25.6 0.7 compare_and_fusion
  26.4 68.8 %all-gather.2.cloned.1.call-done = bf16[12288,512]{1,0:T(8,128)(2,1)} async-done(((bf16[768,512]{1,0:T(8,128)(2,1)}), bf16[12288,512]{1,0:T(8,128)(2,1)}) %all-gather.2.cloned.1.call-update) | async-done | bytes 12582928 | tf_op jit(solution)/shard_map/all_gather | solution.py:77
  95.2 7.4 %gather_fusion = bf16[256,512]{1,0:T(8,128)(2,1)S(1)} fusion(bf16[12288,512]{1,0:T(8,128)(2,1)} %all-gather.2.cloned.1.call-done, s32[1024]{0:T(1024)S(1)} %pad_clamp_fusion), kind=kCustom, calls=%fused_computation | custom fusion | bytes 525312 | tf_op jit(solution)/shard_map/gather | solution.py:79
  102.6 0.2 convert_reduce_fusion
  102.8 0.2 fusion.38
  103.1 2.8 fusion.76
  105.9 0.8 slice_bitcast_fusion
  106.6 0.1 copy.40
  106.8 0.1 copy.41
  107.0 1.6 divide_convert_fusion
  108.5 0.3 fusion.78
  108.9 0.1 fusion.40
  109.0 0.3 copy-done.2
  109.3 0.2 copy.35
  109.5 1.7 multiply_reduce_fusion.1
  111.3 2.1 fusion.75
  113.3 0.1 broadcast_add_fusion
  113.4 0.1 copy.36
  113.6 2.0 fusion.26
  115.7 0.2 fusion.80
  115.9 1.0 fusion.79
  116.9 0.9 fusion.81
  117.9 0.1 copy.37
  118.0 1.8 copy.38
  119.8 1.8 copy.39
  121.6 3.4 multiply_reduce_fusion
  125.0 1.0 fusion.74
  126.0 2.9 scatter_custom_fusion.1
  128.9 4.3 all-to-all-start.1
  133.2 0.2 all-reduce.9.cloned.1.call-start
  133.4 2.5 fusion.45
  136.0 0.5 broadcast.379
  136.5 0.7 reduce.15
  137.3 13.3 %all-to-all-done.1 = bf16[16,32,512]{2,1,0:T(8,128)(2,1)} async-done(((bf16[16,32,512]{2,1,0:T(8,128)(2,1)}), bf16[16,32,512]{2,1,0:T(8,128)(2,1)}, u32[]{:S(2)}, u32[]{:S(2)}) %all-to-all-start.1) | async-done | bytes 524320 | tf_op jit(solution)/shard_map/all_to_all | solution.py:95
  150.6 5.5 scatter_custom_fusion.2
  156.2 256.1 %all-reduce.9.cloned.1.call-done = f32[512,512]{1,0:T(8,128)} async-done(((f32[512,512]{1,0:T(8,128)}), f32[512,512]{1,0:T(8,128)}) %all-reduce.9.cloned.1.call-update) | async-done | bytes 1048592 | tf_op jit(solution)/shard_map/psum | solution.py:110
  412.3 2.1 multiply_convert_fusion
  414.4 156.7 %all-reduce.7.cloned.1.call-done = f32[768,512]{1,0:T(8,128)} async-done(((f32[768,512]{1,0:T(8,128)}), f32[768,512]{1,0:T(8,128)}) %all-reduce.7.cloned.1.call-update) | async-done | bytes 1572880 | tf_op jit(solution)/shard_map/psum | solution.py:109
  571.1 2.7 copy.58
  (36 shorter events, 0.4 us)
Async XLA Ops:
  7.2 95.9 %copy-start = (bf16[512,2048]{1,0:T(8,128)(2,1)S(1)}, bf16[512,2048]{1,0:T(8,128)(2,1)}, u32[]{:S(2)}) copy-start(bf16[512,2048]{1,0:T(8,128)(2,1)} %param.11) | copy-start | bytes 6291460
  7.2 88.0 %all-gather.2.cloned.1.call-start = ((), (), s32[]{:S(2)}) async-start(), calls=%async_computation.2 | async-start | bytes 13369344 | tf_op jit(solution)/shard_map/all_gather | solution.py:77
  13.1 115.8 %all-to-all-start = ((s32[16,1,32]{2,1,0:T(1,128)}), s32[16,1,32]{2,1,0:T(1,128)S(1)}, u32[]{:S(2)}, u32[]{:S(2)}) async-start(s32[16,1,32]{2,1,0:T(1,128)} %all_to_all.9), calls=%async_computation | async-start | bytes 16384 | tf_op jit(solution)/shard_map/all_to_all | solution.py:73
  106.8 1.8 copy-start.4
  106.9 1.6 copy-start.6
  106.9 1.6 copy-start.8
  108.5 0.8 copy-start.2
  113.6 2.1 copy-start.5
  113.6 2.3 copy-start.7
  115.6 1.3 copy-start.3
  121.6 4.4 copy-start.1
  128.9 21.7 %all-to-all-start.1 = ((bf16[16,32,512]{2,1,0:T(8,128)(2,1)}), bf16[16,32,512]{2,1,0:T(8,128)(2,1)}, u32[]{:S(2)}, u32[]{:S(2)}) async-start(bf16[16,32,512]{2,1,0:T(8,128)(2,1)} %bitcast.120), calls=%async_computation.1 | async-start | bytes 1048576 | tf_op jit(solution)/shard_map/all_to_all | solution.py:95
  133.2 279.0 %all-reduce.9.cloned.1.call-start = ((), (), s32[]{:S(2)}) async-start(), calls=%async_computation.4 | async-start | bytes 2097152 | tf_op jit(solution)/shard_map/psum | solution.py:110
  136.0 435.1 %all-reduce.7.cloned.1.call-start = ((), (), s32[]{:S(2)}) async-start(), calls=%async_computation.3 | async-start | bytes 3145728 | tf_op jit(solution)/shard_map/psum | solution.py:109
Sparse Core Ops, SparseCore 0:
  10.1 84.9 all-gather.1
  139.1 273.0 all-reduce.8
  416.6 154.4 all-reduce.6
where the time goes:
time: 584 us; the launch traced here: 580 us
  waiting for transfers between devices  496 us (85%)
  local copies, waits for them, and re-layouts  18.5 us (3%)
  other arithmetic  18.5 us (3%)
  matrix products  16.5 us (3%)
  starting transfers between devices  16.4 us (3%)
  between operations  14.6 us (2%)
    psum x1, waiting for transfers between devices, per_device(): dense_total = lax.psum(dense_part, ('dp', 'table'))  256 us
    psum x1, waiting for transfers between devices, per_device(): table_grad = lax.psum(local_grad, 'dp')  157 us
    all_gather x1, waiting for transfers between devices, per_device(): piece = lax.all_gather(table, 'table', axis=0, tiled=True)  68.8 us
    all_to_all x1, waiting for transfers between devices, per_device(): lax.all_to_all(outgoing.reshape(groups, capacity, model_width), 'table',...  13.3 us
    all_to_all x1, starting transfers between devices, per_device(): lax.all_to_all(requested, 'table', split_axis=0, concat_axis=0, tiled=True)  11.8 us
  transfers between devices with their start and end apart: 5, of which 4 were waited for; matrix products, arithmetic and copies ran while one was open for 9% of the time, Pallas kernels for 0%

commit v1 on v0

--- a/solution.py
+++ b/solution.py
@@ -53,10 +53,15 @@
     return (output, mixed)
 
 
+def pick_rows(index, length):
+    return (index[:, None] == jnp.arange(length, dtype=jnp.int32)[None, :]).astype(jnp.bfloat16)
+
+
 def per_device(table, history_shard, history_row, lengths, w_in, w_out, cotangent):
     shard_rows, model_width = table.shape
     samples_here, seq_span = history_row.shape
     groups = lax.axis_size("table")
+    copies = lax.axis_size("dp")
     slot_count = samples_here * seq_span
     capacity = 2 * slot_count // groups
     owners = history_shard[:, :, 0].reshape(-1)
@@ -64,20 +69,21 @@
     owner_hits = (owners[:, None] == jnp.arange(groups)[None, :]).astype(jnp.int32)
     slot_rank = jnp.sum((jnp.cumsum(owner_hits, axis=0) - owner_hits) * owner_hits, axis=1)
     position = owners * capacity + slot_rank
-    requested = (
-        jnp.zeros((groups * capacity,), jnp.int32)
-        .at[position]
-        .set(local_rows)
-        .reshape(groups, capacity)
+    slot_hits = position[:, None] == jnp.arange(groups * capacity, dtype=jnp.int32)[None, :]
+    requested = jnp.sum(jnp.where(slot_hits, local_rows[:, None], 0), axis=0).reshape(
+        groups, capacity
     )
     incoming = lax.all_to_all(requested, "table", split_axis=0, concat_axis=0, tiled=True).reshape(
         -1
     )
-    global_rows = owners * shard_rows + local_rows
-    piece = lax.all_gather(table, "table", axis=0, tiled=True)
-    inside = (global_rows >= 0) & (global_rows < piece.shape[0])
-    taken = piece[jnp.clip(global_rows, 0, piece.shape[0] - 1)].astype(jnp.float32)
-    embedded = jnp.where(inside[:, None], taken, 0.0).astype(jnp.bfloat16)
+    reply = jnp.dot(
+        pick_rows(incoming, shard_rows), table, preferred_element_type=jnp.float32
+    ).astype(jnp.bfloat16)
+    received = lax.all_to_all(
+        reply.reshape(groups, capacity, model_width), "table", split_axis=0, concat_axis=0, tiled=True
+    ).reshape(groups * capacity, model_width)
+    place = slot_hits.astype(jnp.bfloat16)
+    embedded = jnp.dot(place, received, preferred_element_type=jnp.float32).astype(jnp.bfloat16)
     embedded = embedded.reshape(samples_here, seq_span, model_width)
     output, pullback, mixed = jax.vjp(
         lambda rows_in: hstu_layer(rows_in, w_in, w_out, lengths), embedded, has_aux=True
@@ -85,30 +91,55 @@
     row_live = jnp.arange(seq_span)[None, :] < lengths[:, None]
     grad_seed = jnp.where(row_live[:, :, None], cotangent, jnp.zeros_like(cotangent))
     flat_seed = grad_seed.reshape(-1, model_width)
+
+    total_slots = slot_count * copies * groups
+    grad_scale = 1.0 / math.sqrt(total_slots)
+    dense_part = lax.dot_general(
+        mixed, flat_seed, (((0,), (0,)), ((), ())), preferred_element_type=jnp.float32
+    ).astype(jnp.bfloat16)
+    dense_rows = model_width // groups
+    dense_terms = lax.all_to_all(
+        dense_part.reshape(groups, dense_rows, model_width),
+        "table",
+        split_axis=0,
+        concat_axis=0,
+        tiled=True,
+    )
+    dense_block = jnp.sum(dense_terms.astype(jnp.float32), axis=0).astype(jnp.bfloat16)
+    dense_blocks = lax.all_gather(dense_block, "dp", axis=0, tiled=False)
+    dense_sum = jnp.sum(dense_blocks.astype(jnp.float32), axis=0) * grad_scale
+    dense_grad = lax.all_gather(dense_sum.astype(jnp.bfloat16), "table", axis=0, tiled=True)
+
     (row_grad,) = pullback(flat_seed.astype(jnp.float32))
-    dense_part = jnp.dot(mixed.T, flat_seed, preferred_element_type=jnp.float32)
-    outgoing = (
-        jnp.zeros((groups * capacity, model_width), jnp.bfloat16)
-        .at[position]
-        .set(row_grad.reshape(-1, model_width))
-    )
+    outgoing = lax.dot_general(
+        place,
+        row_grad.reshape(-1, model_width),
+        (((0,), (0,)), ((), ())),
+        preferred_element_type=jnp.float32,
+    ).astype(jnp.bfloat16)
     arrived = lax.all_to_all(
         outgoing.reshape(groups, capacity, model_width),
         "table",
         split_axis=0,
         concat_axis=0,
         tiled=True,
+    ).reshape(groups * capacity, model_width)
+    local_grad = lax.dot_general(
+        pick_rows(incoming, shard_rows),
+        arrived,
+        (((0,), (0,)), ((), ())),
+        preferred_element_type=jnp.float32,
+    ).astype(jnp.bfloat16)
+    part_rows = shard_rows // copies
+    terms = lax.all_to_all(
+        local_grad.reshape(copies, part_rows, model_width),
+        "dp",
+        split_axis=0,
+        concat_axis=0,
+        tiled=True,
     )
-    local_grad = (
-        jnp.zeros((shard_rows, model_width), jnp.float32)
-        .at[incoming]
-        .add(arrived.reshape(-1, model_width).astype(jnp.float32))
-    )
-    total_slots = slot_count * lax.axis_size("dp") * groups
-    grad_scale = 1.0 / math.sqrt(total_slots)
-    table_grad = lax.psum(local_grad, "dp")
-    dense_total = lax.psum(dense_part, ("dp", "table"))
-    dense_grad = (dense_total * grad_scale).astype(jnp.bfloat16)
+    summed = jnp.sum(terms.astype(jnp.float32), axis=0).astype(jnp.bfloat16)
+    table_grad = lax.all_gather(summed, "dp", axis=0, tiled=True).astype(jnp.float32)
     return (table_grad, dense_grad)
 
 

time: 584 us -> 226 us (0.39)
  waiting for transfers between devices: 496 us -> 43.2 us
  blocking collectives: 0 us -> 116 us
  local copies, waits for them, and re-layouts: 18.5 us -> 8.98 us
  other arithmetic: 18.5 us -> 10.8 us
    psum x2 -> x0, waiting for transfers between devices: 413 us -> none  [the longest x1 256 us: per_device(): dense_total = lax.psum(dense_part, ('dp', 'table'))]
    all_gather x1, waiting for transfers between devices: 68.8 us -> 0.01 us  [per_device(): dense_blocks = lax.all_gather(dense_block, 'dp', axis=0, tiled=False)]
    all_gather x0 -> x2, blocking collectives: none -> 65.6 us  [the longest x1 40.4 us: per_device(): lax.all_gather(summed, 'dp', axis=0, tiled=True).astype(jnp.float32)]
    all_to_all x0 -> x2, blocking collectives: none -> 50.2 us  [the longest x1 31.6 us: per_device(): lax.all_to_all(local_grad.reshape(copies, part_rows, model_width), 'dp',...]
    all_to_all x1 -> x2, waiting for transfers between devices: 0.01 us -> 28.3 us  [the longest x1 16.6 us: per_device(): lax.all_to_all(reply.reshape(groups, capacity, model_width), 'table', spl...]
    gather x1 -> x0, local copies, waits for them, and re-layouts: 7.4 us -> none  [per_device(): piece[jnp.clip(global_rows, 0, piece.shape[0] - 1)].astype(jnp.float32)]
    all_to_all x1 -> x2, starting transfers between devices: 11.8 us -> 8.15 us  [the longest x1 4.13 us: per_device(): lax.all_to_all(dense_part.reshape(groups, dense_rows, model_width), 'tabl...]
  transfers between devices with their start and end apart: 5 -> 4, of which waited for: 4 -> 3; matrix products, arithmetic and copies ran while one was open for 9% -> 4% of each run, Pallas kernels for 0% -> 0%
where the time goes in v1:
time: 226 us
  blocking collectives  116 us (51%)
  waiting for transfers between devices  43.2 us (19%)
  matrix products  20.1 us (9%)
  between operations  14.9 us (7%)
  starting transfers between devices  11.7 us (5%)
  other arithmetic  10.8 us (5%)
  local copies, waits for them, and re-layouts  8.98 us (4%)
    all_gather x1, blocking collectives, per_device(): lax.all_gather(summed, 'dp', axis=0, tiled=True).astype(jnp.float32)  40.4 us
    all_to_all x1, blocking collectives, per_device(): lax.all_to_all(local_grad.reshape(copies, part_rows, model_width), 'dp',...  31.6 us
    all_gather x1, blocking collectives, per_device(): lax.all_gather(dense_sum.astype(jnp.bfloat16), 'table', axis=0, tiled=True)  25.2 us
    all_to_all x1, blocking collectives, per_device(): lax.all_to_all(requested, 'table', split_axis=0, concat_axis=0, tiled=True)  18.6 us
    all_to_all x1, waiting for transfers between devices, per_device(): lax.all_to_all(reply.reshape(groups, capacity, model_width), 'table', spl...  16.6 us
    all_to_all x1, waiting for transfers between devices, per_device(): lax.all_to_all(outgoing.reshape(groups, capacity, model_width), 'table',...  14.9 us
    all_to_all x1, waiting for transfers between devices, per_device(): lax.all_to_all(dense_part.reshape(groups, dense_rows, model_width), 'tabl...  11.7 us
    dot_general x2, matrix products, hstu_layer(): jnp.dot(normed.reshape(samples_here * seq_span, model_width), w_in, prefe...  5.66 us
  transfers between devices with their start and end apart: 4, of which 3 were waited for; matrix products, arithmetic and copies ran while one was open for 4% of the time, Pallas kernels for 0%

profile of v1, /device:TPU:1, one launch (start us, length us, event | category | flops | bytes accessed | tf_op | source)
XLA Modules:
  0.0 225.5 jit_solution(14855246301839063184)
XLA Ops:
  7.2 0.8 fusion.62
  8.0 0.6 reduce-window.6
  8.6 0.2 slice_reduce_fusion
  8.8 0.8 fusion.61
  9.6 0.7 multiply_add_fusion.2
  10.3 0.8 select_reduce_fusion
  11.2 18.6 %all_to_all.29 = s32[16,1,32]{2,1,0:T(1,128)S(1)} all-to-all(s32[16,1,32]{2,1,0:T(1,128)S(1)} %all_to_all.18), channel_id=1, replica_groups=mesh['dp'=32,'table'=16] {'table'}, dimensions={0} | all-to-all | bytes 4096 | tf_op jit(solution)/shard_map/all_to_all | solution.py:76
  29.8 0.5 broadcast.199
  30.3 0.7 reduce.19
  31.1 2.5 %fusion.17 = bf16[512,512]{1,0:T(8,128)(2,1)} fusion(bf16[768,512]{1,0:T(8,128)(2,1)} %param.7, s32[512]{0:T(512)S(1)} %eq.68), kind=kOutput, calls=%fused_computation.23 | convolution fusion | flops 403308544 | bytes 1312768 | tf_op jit(solution)/shard_map/dot_general | solution.py:79
  33.6 4.0 %all-to-all-start.1 = ((bf16[16,32,512]{2,1,0:T(8,128)(2,1)}), bf16[16,32,512]{2,1,0:T(8,128)(2,1)S(1)}, u32[]{:S(2)}, u32[]{:S(2)}) async-start(bf16[16,32,512]{2,1,0:T(8,128)(2,1)} %bitcast.6), calls=%async_computation.1 | async-start | bytes 1048576 | tf_op jit(solution)/shard_map/all_to_all | solution.py:82
  38.4 16.6 %all-to-all-done.1 = bf16[16,32,512]{2,1,0:T(8,128)(2,1)S(1)} async-done(((bf16[16,32,512]{2,1,0:T(8,128)(2,1)}), bf16[16,32,512]{2,1,0:T(8,128)(2,1)S(1)}, u32[]{:S(2)}, u32[]{:S(2)}) %all-to-all-start.1) | async-done | bytes 524320 | tf_op jit(solution)/shard_map/all_to_all | solution.py:82
  55.0 0.4 fusion.72
  55.4 0.2 multiply_reduce_fusion.2
  55.7 2.7 %fusion.70 = (bf16[256,2048]{1,0:T(8,128)(2,1)S(1)}, f32[256,2048]{1,0:T(8,128)}, f32[256,2048]{1,0:T(8,128)}) fusion(bf16[512,2048]{1,0:T(8,128)(2,1)S(1)} %copy-done, f32[256,512]{1,0:T(8,128)S(1)} %get-tuple-element.15, f32[256]{0:T(256)S(1)} %fusion.63, f32[256]{0:T(256)S(1)} %broadcast_multiply_fusion.1), kind=kOutput, calls=%fused_computation.113 | convolution fusion | flops 539885568 | bytes 7866368 | tf_op jit(solution)/shard_map/jvp()/dot_general | solution.py:23
  58.4 0.8 slice_bitcast_fusion
  59.3 0.1 copy.53
  59.5 0.6 copy-done.5
  60.0 1.6 divide_convert_fusion
  61.6 0.3 fusion.73
  62.1 0.3 copy-done.3
  62.4 0.4 copy-done.1
  62.7 1.2 copy.48
  64.0 1.8 multiply_reduce_fusion.1
  65.9 1.3 convolution_convert_fusion.1
  67.2 1.0 fusion.69
  68.4 1.3 fusion.76
  69.7 2.0 fusion.31
  71.8 0.3 fusion.74
  72.1 0.9 fusion.75
  73.0 0.8 copy.52
  73.9 1.9 copy.50
  75.7 0.9 copy.51
  76.6 4.1 %all-to-all-start.4 = ((bf16[16,32,512]{2,1,0:T(8,128)(2,1)}), bf16[16,32,512]{2,1,0:T(8,128)(2,1)}, u32[]{:S(2)}, u32[]{:S(2)}) async-start(bf16[16,32,512]{2,1,0:T(8,128)(2,1)} %bitcast.30), calls=%async_computation.4 | async-start | bytes 1048576 | tf_op jit(solution)/shard_map/all_to_all | solution.py:101
  80.7 2.9 %multiply_reduce_fusion = (f32[256]{0:T(256)S(1)}, f32[256,512]{1,0:T(8,128)S(1)}) fusion(f32[256,512]{1,0:T(8,128)S(1)} %get-tuple-element.15, f32[256]{0:T(256)S(1)} %broadcast_multiply_fusion.1, bf16[512,2048]{1,0:T(8,128)(2,1)S(1)} %copy-done, f32[256,2048]{1,0:T(8,128)} %get-tuple-element.16, f32[256,512]{1,0:T(8,128)} %get-tuple-element.8, ...), kind=kOutput, calls=%fused_computation.56 | convolution fusion | flops 545390336 | bytes 6555648 | tf_op jit(solution)/shard_map/transpose(jvp())/dot_general | solution.py:23
  83.7 0.3 fusion.68
  84.0 1.3 convolution_convert_fusion.2
  85.3 11.7 %all-to-all-done.4 = bf16[16,32,512]{2,1,0:T(8,128)(2,1)} async-done(((bf16[16,32,512]{2,1,0:T(8,128)(2,1)}), bf16[16,32,512]{2,1,0:T(8,128)(2,1)}, u32[]{:S(2)}, u32[]{:S(2)}) %all-to-all-start.4) | async-done | bytes 524320 | tf_op jit(solution)/shard_map/all_to_all | solution.py:101
  96.9 3.5 %all-to-all-start.2 = ((bf16[16,32,512]{2,1,0:T(8,128)(2,1)}), bf16[16,32,512]{2,1,0:T(8,128)(2,1)S(1)}, u32[]{:S(2)}, u32[]{:S(2)}) async-start(bf16[16,32,512]{2,1,0:T(8,128)(2,1)} %bitcast.27), calls=%async_computation.2 | async-start | bytes 1048576 | tf_op jit(solution)/shard_map/all_to_all | solution.py:120
  100.5 1.7 reduce_sum.150
  102.2 14.9 %all-to-all-done.2 = bf16[16,32,512]{2,1,0:T(8,128)(2,1)S(1)} async-done(((bf16[16,32,512]{2,1,0:T(8,128)(2,1)}), bf16[16,32,512]{2,1,0:T(8,128)(2,1)S(1)}, u32[]{:S(2)}, u32[]{:S(2)}) %all-to-all-start.2) | async-done | bytes 524320 | tf_op jit(solution)/shard_map/all_to_all | solution.py:120
  117.1 0.7 fusion.16
  117.8 31.6 %all_to_all.30 = bf16[32,24,512]{2,1,0:T(8,128)(2,1)S(1)} all-to-all(bf16[32,24,512]{2,1,0:T(8,128)(2,1)S(1)} %bitcast.113), channel_id=1, replica_groups=mesh['dp'=32,'table'=16] {'dp'}, dimensions={0} | all-to-all | bytes 1572864 | tf_op jit(solution)/shard_map/all_to_all | solution.py:134
  149.5 40.4 %all_gather.12 = bf16[768,512]{1,0:T(8,128)(2,1)S(1)} all-gather(bf16[24,512]{1,0:T(8,128)(2,1)S(1)} %reduce_sum.149), channel_id=1, replica_groups=mesh['dp'=32,'table'=16] {'dp'}, dimensions={0}, use_global_device_ids=true | all-gather | bytes 811008 | tf_op jit(solution)/shard_map/all_gather | solution.py:142
  189.9 1.4 convert_element_type.164
  191.3 1.4 convert_reduce_fusion
  192.7 25.2 %all_gather.15 = bf16[512,512]{1,0:T(8,128)(2,1)S(1)} all-gather(bf16[32,512]{1,0:T(8,128)(2,1)S(1)} %multiply_convert_fusion.4), channel_id=1, replica_groups=mesh['dp'=32,'table'=16] {'table'}, dimensions={0}, use_global_device_ids=true | all-gather | bytes 557056 | tf_op jit(solution)/shard_map/all_gather | solution.py:111
  217.9 0.8 copy.70
  (41 shorter events, 1.1 us)
Async XLA Ops:
  7.2 48.5 %copy-start = (bf16[512,2048]{1,0:T(8,128)(2,1)S(1)}, bf16[512,2048]{1,0:T(8,128)(2,1)}, u32[]{:S(2)}) copy-start(bf16[512,2048]{1,0:T(8,128)(2,1)} %param.11) | copy-start | bytes 6291460
  33.6 21.4 %all-to-all-start.1 = ((bf16[16,32,512]{2,1,0:T(8,128)(2,1)}), bf16[16,32,512]{2,1,0:T(8,128)(2,1)S(1)}, u32[]{:S(2)}, u32[]{:S(2)}) async-start(bf16[16,32,512]{2,1,0:T(8,128)(2,1)} %bitcast.6), calls=%async_computation.1 | async-start | bytes 1048576 | tf_op jit(solution)/shard_map/all_to_all | solution.py:82
  59.3 0.7 copy-start.5
  59.4 2.1 copy-start.7
  60.0 1.6 copy-start.9
  61.6 0.8 copy-start.3
  61.6 2.4 %copy-start.2 = (bf16[1,256,512]{2,1,0:T(8,128)(2,1)S(1)}, bf16[1,256,512]{2,1,0:T(8,128)(2,1)}, u32[]{:S(2)}) copy-start(bf16[1,256,512]{2,1,0:T(8,128)(2,1)} %param.13) | copy-start | bytes 786436
  61.9 0.8 copy-start.1
  64.0 1.9 copy-start.4
  69.7 2.1 copy-start.6
  69.7 2.4 %copy-start.8 = (bf16[256,512]{0,1:T(8,128)(2,1)S(1)}, bf16[256,512]{0,1:T(8,128)(2,1)}, u32[]{:S(2)}) copy-start(bf16[256,512]{0,1:T(8,128)(2,1)} %copy-done.7) | copy-start | bytes 786436
  73.9 6.9 %copy-start.10 = (bf16[256,512]{1,0:T(8,128)(2,1)S(1)}, bf16[256,512]{1,0:T(8,128)(2,1)}, u32[]{:S(2)}) copy-start(bf16[256,512]{1,0:T(8,128)(2,1)} %copy.52) | copy-start | bytes 786436
  76.6 20.3 %all-to-all-start.4 = ((bf16[16,32,512]{2,1,0:T(8,128)(2,1)}), bf16[16,32,512]{2,1,0:T(8,128)(2,1)}, u32[]{:S(2)}, u32[]{:S(2)}) async-start(bf16[16,32,512]{2,1,0:T(8,128)(2,1)} %bitcast.30), calls=%async_computation.4 | async-start | bytes 1048576 | tf_op jit(solution)/shard_map/all_to_all | solution.py:101
  96.9 20.2 %all-to-all-start.2 = ((bf16[16,32,512]{2,1,0:T(8,128)(2,1)}), bf16[16,32,512]{2,1,0:T(8,128)(2,1)S(1)}, u32[]{:S(2)}, u32[]{:S(2)}) async-start(bf16[16,32,512]{2,1,0:T(8,128)(2,1)} %bitcast.27), calls=%async_computation.2 | async-start | bytes 1048576 | tf_op jit(solution)/shard_map/all_to_all | solution.py:120
  100.4 90.9 %all-gather.3.cloned.1.call-start = ((), (), s32[]{:S(2)}) async-start(), calls=%async_computation.5 | async-start | bytes 1081344 | tf_op jit(solution)/shard_map/all_gather | solution.py:109
Sparse Core Ops, SparseCore 0:
  104.4 79.3 all-gather.2

commit v2 on v1

--- a/solution.py
+++ b/solution.py
@@ -1,11 +1,17 @@
+import functools
 import math
 
 import jax
 import jax.numpy as jnp
 from jax import lax
+from jax.experimental import pallas as pl
+from jax.experimental.pallas import tpu as pltpu
 from jax.sharding import PartitionSpec as P
 
 HEADS = 4
+NX = 4
+NY = 8
+MESH = pl.DeviceIdType.MESH
 
 
 def layer_norm(values):
@@ -55,6 +61,338 @@
 
 def pick_rows(index, length):
     return (index[:, None] == jnp.arange(length, dtype=jnp.int32)[None, :]).astype(jnp.bfloat16)
+
+
+def send(src, dst, send_sem, recv_sem, **where):
+    return pltpu.make_async_remote_copy(
+        src_ref=src,
+        dst_ref=dst,
+        send_sem=send_sem,
+        recv_sem=recv_sem,
+        device_id=where,
+        device_id_type=MESH,
+    )
+
+
+def each(start, stop, body):
+    def step(i, carry):
+        body(i)
+        return carry
+
+    lax.fori_loop(start, stop, step, 0)
+
+
+def exchange_kernel(
+    scale,
+    outgoing,
+    dense_part,
+    incoming,
+    table_out,
+    dense_out,
+    arrived,
+    dense_arr,
+    part,
+    x_in,
+    x_sum,
+    y_in,
+    whole,
+    dx_out,
+    dx_in,
+    dy_in,
+    d_row,
+    d_all,
+    z_s,
+    z_r,
+    dz_s,
+    dz_r,
+    x_s,
+    x_r,
+    y_s,
+    y_r,
+    gy_s,
+    gy_r,
+    gx_s,
+    gx_r,
+    dx_s,
+    dx_r,
+    dy_s,
+    dy_r,
+    dgx_s,
+    dgx_r,
+    dgz_s,
+    dgz_r,
+):
+    nz, cap, width = outgoing.shape
+    rows = table_out.shape[0]
+    x_rows = rows // NX
+    half = x_rows // 2
+    me = lax.axis_index("table")
+    spot = lax.axis_index("dp")
+    x = spot // NY
+    y = lax.rem(spot, NY)
+    f32, bf16 = jnp.float32, jnp.bfloat16
+
+    def zp(k):
+        return lax.rem(me + k, nz)
+
+    def xp(k):
+        return lax.rem(x + k, NX)
+
+    def yp(k):
+        return lax.rem(y + k, NY)
+
+    def at_x(px):
+        return px * NY + y
+
+    def at_y(py):
+        return x * NY + py
+
+    barrier = pltpu.get_barrier_semaphore()
+
+    def greet(axis, peer):
+        pl.semaphore_signal(barrier, inc=1, device_id={axis: peer}, device_id_type=MESH)
+
+    each(1, nz, lambda k: greet("table", zp(k)))
+    each(1, NX, lambda k: greet("dp", at_x(xp(k))))
+    each(1, NY, lambda k: greet("dp", at_y(yp(k))))
+    pl.semaphore_wait(barrier, nz - 1 + NX - 1 + NY - 1)
+
+    def z_copy(p):
+        return send(outgoing.at[p], arrived.at[me], z_s.at[p], z_r.at[me], table=p)
+
+    def z_wait(p):
+        send(outgoing.at[p], arrived.at[p], z_s.at[p], z_r.at[p], table=p).wait_recv()
+
+    def dz_copy(p):
+        return send(dense_part.at[p], dense_arr.at[me], dz_s.at[p], dz_r.at[me], table=p)
+
+    def dz_wait(p):
+        send(dense_part.at[p], dense_arr.at[p], dz_s.at[p], dz_r.at[p], table=p).wait_recv()
+
+    each(1, nz, lambda k: z_copy(zp(k)).start())
+    each(1, nz, lambda k: dz_copy(zp(k)).start())
+    arrived[me] = outgoing[me]
+    dense_arr[me] = dense_part[me]
+    each(1, nz, lambda k: z_wait(zp(k)))
+
+    def x_copy(p, c):
+        return send(part.at[p, c], x_in.at[x, c], x_s.at[p, c], x_r.at[x, c], dp=at_x(p))
+
+    def x_wait(p, c):
+        send(part.at[p, c], x_in.at[p, c], x_s.at[p, c], x_r.at[p, c], dp=at_x(p)).wait_recv()
+
+    def make_part(p):
+        line = lax.broadcasted_iota(jnp.int32, (x_rows, nz * cap), 0) + p * x_rows
+        pick = (line == incoming[...]).astype(f32).astype(bf16)
+        got = arrived[...].reshape(nz * cap, width)
+        block = jnp.dot(pick, got, preferred_element_type=f32).astype(bf16)
+        for c in range(NY):
+            part[p, c] = block[
+                (c % 2) * half : (c % 2 + 1) * half, (c // 2) * 128 : (c // 2 + 1) * 128
+            ]
+
+    def x_stage(k):
+        p = xp(k)
+        make_part(p)
+        each(1, NY + 1, lambda j: x_copy(p, yp(j)).start())
+
+    each(1, NX, x_stage)
+    make_part(x)
+
+    def y_copy(c):
+        return send(x_sum.at[c], y_in.at[y], y_s.at[c], y_r.at[y], dp=at_y(c))
+
+    def y_wait(c):
+        send(x_sum.at[c], y_in.at[c], y_s.at[c], y_r.at[c], dp=at_y(c)).wait_recv()
+
+    def sum_x(c):
+        total = part[x, c].astype(f32)
+        for k in range(1, NX):
+            p = xp(k)
+            x_wait(p, c)
+            total = total + x_in[p, c].astype(f32)
+        x_sum[c] = total.astype(bf16)
+
+    def y_stage(j):
+        c = yp(j)
+        sum_x(c)
+        y_copy(c).start()
+
+    each(1, NY, y_stage)
+    sum_x(y)
+
+    def dx_copy(p):
+        return send(dx_out.at[p], dx_in.at[x], dx_s.at[p], dx_r.at[x], dp=at_x(p))
+
+    def dx_wait(p):
+        send(dx_out.at[p], dx_in.at[p], dx_s.at[p], dx_r.at[p], dp=at_x(p)).wait_recv()
+
+    each(1, nz, lambda k: dz_wait(zp(k)))
+    dense_sum = dense_arr[0].astype(f32)
+    for k in range(1, nz):
+        dense_sum = dense_sum + dense_arr[k].astype(f32)
+    dense_sum = dense_sum.astype(bf16)
+    for c in range(NX):
+        dx_out[c] = dense_sum[:, c * 128 : (c + 1) * 128]
+    each(1, NX, lambda k: dx_copy(xp(k)).start())
+
+    total = x_sum[y].astype(f32)
+    for j in range(1, NY):
+        c = yp(j)
+        y_wait(c)
+        total = total + y_in[c].astype(f32)
+    whole[x, y] = total.astype(bf16)
+
+    def gy_copy(p):
+        return send(whole.at[x, y], whole.at[x, y], gy_s.at[p], gy_r.at[y], dp=at_y(p))
+
+    def gy_wait(p):
+        send(whole.at[x, p], whole.at[x, p], gy_s.at[p], gy_r.at[p], dp=at_y(p)).wait_recv()
+
+    def gx_copy(p, c):
+        return send(whole.at[x, c], whole.at[x, c], gx_s.at[p, c], gx_r.at[x, c], dp=at_x(p))
+
+    def gx_wait(p, c):
+        send(whole.at[p, c], whole.at[p, c], gx_s.at[p, c], gx_r.at[p, c], dp=at_x(p)).wait_recv()
+
+    each(1, NY, lambda k: gy_copy(yp(k)).start())
+    each(1, NX, lambda k: gx_copy(xp(k), y).start())
+
+    def dy_copy(p):
+        return send(dy_in.at[y], dy_in.at[y], dy_s.at[p], dy_r.at[y], dp=at_y(p))
+
+    def dy_wait(p):
+        send(dy_in.at[p], dy_in.at[p], dy_s.at[p], dy_r.at[p], dp=at_y(p)).wait_recv()
+
+    dx_in[x] = dx_out[x]
+    each(1, NX, lambda k: dx_wait(xp(k)))
+    d_total = dx_in[0].astype(f32)
+    for k in range(1, NX):
+        d_total = d_total + dx_in[k].astype(f32)
+    dy_in[y] = d_total.astype(bf16)
+    each(1, NY, lambda k: dy_copy(yp(k)).start())
+
+    def pass_on(j):
+        c = yp(j)
+        gy_wait(c)
+        each(1, NX, lambda k: gx_copy(xp(k), c).start())
+
+    each(1, NY // 2, pass_on)
+
+    def dgx_copy(p):
+        return send(d_row.at[x], d_row.at[x], dgx_s.at[p], dgx_r.at[x], dp=at_x(p))
+
+    def dgx_wait(p):
+        send(d_row.at[p], d_row.at[p], dgx_s.at[p], dgx_r.at[p], dp=at_x(p)).wait_recv()
+
+    each(1, NY, lambda k: dy_wait(yp(k)))
+    d_total = dy_in[0].astype(f32)
+    for k in range(1, NY):
+        d_total = d_total + dy_in[k].astype(f32)
+    d_row[x] = (d_total * scale).astype(bf16)
+    each(1, NX, lambda k: dgx_copy(xp(k)).start())
+    each(NY // 2, NY, pass_on)
+
+    def dgz_copy(p):
+        return send(d_row, d_all.at[me], dgz_s.at[p], dgz_r.at[me], table=p)
+
+    def dgz_wait(p):
+        send(d_row, d_all.at[p], dgz_s.at[p], dgz_r.at[p], table=p).wait_recv()
+
+    each(1, NX, lambda k: dgx_wait(xp(k)))
+    each(1, nz, lambda k: dgz_copy(zp(k)).start())
+    d_all[me] = d_row[...]
+
+    def gx_wait_all(k):
+        each(0, NY, lambda c: gx_wait(xp(k), c))
+
+    each(1, NX, gx_wait_all)
+    for px in range(NX):
+        for c in range(NY):
+            table_out[
+                px * x_rows + (c % 2) * half : px * x_rows + (c % 2 + 1) * half,
+                (c // 2) * 128 : (c // 2 + 1) * 128,
+            ] = whole[px, c]
+    each(1, nz, lambda k: dgz_wait(zp(k)))
+    for t in range(nz):
+        for c in range(NX):
+            dense_out[t * cap : (t + 1) * cap, c * 128 : (c + 1) * 128] = d_all[t, c]
+
+    def sent_z(k):
+        p = zp(k)
+        z_copy(p).wait_send()
+        dz_copy(p).wait_send()
+        dgz_copy(p).wait_send()
+
+    def sent_x(k):
+        p = xp(k)
+        dx_copy(p).wait_send()
+        dgx_copy(p).wait_send()
+
+        def pieces(c):
+            x_copy(p, c).wait_send()
+            gx_copy(p, c).wait_send()
+
+        each(0, NY, pieces)
+
+    def sent_y(k):
+        p = yp(k)
+        y_copy(p).wait_send()
+        gy_copy(p).wait_send()
+        dy_copy(p).wait_send()
+
+    each(1, nz, sent_z)
+    each(1, NX, sent_x)
+    each(1, NY, sent_y)
+
+
+def exchange(outgoing, dense_part, incoming, shard_rows, scale):
+    groups, capacity, width = outgoing.shape
+    bf16 = jnp.bfloat16
+    piece = (shard_rows // NX // 2, 128)
+    small = (capacity, 128)
+    vmem = pl.BlockSpec(memory_space=pltpu.VMEM)
+    dma = pltpu.SemaphoreType.DMA
+
+    def pair(*dims):
+        return [dma(dims), dma(dims)]
+
+    return pl.pallas_call(
+        functools.partial(exchange_kernel, scale),
+        out_shape=(
+            jax.ShapeDtypeStruct((shard_rows, width), bf16),
+            jax.ShapeDtypeStruct((groups * capacity, width), bf16),
+        ),
+        in_specs=[vmem] * 3,
+        out_specs=(vmem, vmem),
+        scratch_shapes=[
+            pltpu.VMEM((groups, capacity, width), bf16),
+            pltpu.VMEM((groups, capacity, width), bf16),
+            pltpu.VMEM((NX, NY) + piece, bf16),
+            pltpu.VMEM((NX, NY) + piece, bf16),
+            pltpu.VMEM((NY,) + piece, bf16),
+            pltpu.VMEM((NY,) + piece, bf16),
+            pltpu.VMEM((NX, NY) + piece, bf16),
+            pltpu.VMEM((NX,) + small, bf16),
+            pltpu.VMEM((NX,) + small, bf16),
+            pltpu.VMEM((NY,) + small, bf16),
+            pltpu.VMEM((NX,) + small, bf16),
+            pltpu.VMEM((groups, NX) + small, bf16),
+        ]
+        + pair(groups)
+        + pair(groups)
+        + pair(NX, NY)
+        + pair(NY)
+        + pair(NY)
+        + pair(NX, NY)
+        + pair(NX)
+        + pair(NY)
+        + pair(NX)
+        + pair(groups),
+        compiler_params=pltpu.CompilerParams(
+            collective_id=0, has_side_effects=True, vmem_limit_bytes=32 << 20
+        ),
+    )(outgoing, dense_part, incoming)
 
 
 def per_device(table, history_shard, history_row, lengths, w_in, w_out, cotangent):
@@ -97,19 +435,6 @@
     dense_part = lax.dot_general(
         mixed, flat_seed, (((0,), (0,)), ((), ())), preferred_element_type=jnp.float32
     ).astype(jnp.bfloat16)
-    dense_rows = model_width // groups
-    dense_terms = lax.all_to_all(
-        dense_part.reshape(groups, dense_rows, model_width),
-        "table",
-        split_axis=0,
-        concat_axis=0,
-        tiled=True,
-    )
-    dense_block = jnp.sum(dense_terms.astype(jnp.float32), axis=0).astype(jnp.bfloat16)
-    dense_blocks = lax.all_gather(dense_block, "dp", axis=0, tiled=False)
-    dense_sum = jnp.sum(dense_blocks.astype(jnp.float32), axis=0) * grad_scale
-    dense_grad = lax.all_gather(dense_sum.astype(jnp.bfloat16), "table", axis=0, tiled=True)
-
     (row_grad,) = pullback(flat_seed.astype(jnp.float32))
     outgoing = lax.dot_general(
         place,
@@ -117,29 +442,14 @@
         (((0,), (0,)), ((), ())),
         preferred_element_type=jnp.float32,
     ).astype(jnp.bfloat16)
-    arrived = lax.all_to_all(
+    table_sum, dense_grad = exchange(
         outgoing.reshape(groups, capacity, model_width),
-        "table",
-        split_axis=0,
-        concat_axis=0,
-        tiled=True,
-    ).reshape(groups * capacity, model_width)
-    local_grad = lax.dot_general(
-        pick_rows(incoming, shard_rows),
-        arrived,
-        (((0,), (0,)), ((), ())),
-        preferred_element_type=jnp.float32,
-    ).astype(jnp.bfloat16)
-    part_rows = shard_rows // copies
-    terms = lax.all_to_all(
-        local_grad.reshape(copies, part_rows, model_width),
-        "dp",
-        split_axis=0,
-        concat_axis=0,
-        tiled=True,
-    )
-    summed = jnp.sum(terms.astype(jnp.float32), axis=0).astype(jnp.bfloat16)
-    table_grad = lax.all_gather(summed, "dp", axis=0, tiled=True).astype(jnp.float32)
+        dense_part.reshape(groups, capacity, model_width),
+        incoming.reshape(1, groups * capacity),
+        shard_rows,
+        grad_scale,
+    )
+    table_grad = table_sum.astype(jnp.float32)
     return (table_grad, dense_grad)
 
 

time: 226 us -> 143 us (0.63)
  blocking collectives: 116 us -> 18.6 us
  Pallas kernels: 0 us -> 66 us
  waiting for transfers between devices: 43.2 us -> 16.6 us
  between operations: 14.9 us -> 1.51 us
  starting transfers between devices: 11.7 us -> 4.02 us
  other arithmetic: 10.8 us -> 7.55 us
    pallas_call x0 -> x1, Pallas kernels: none -> 66 us  [exchange(): pl.pallas_call(functools.partial(exchange_kernel, scale), out_shape=(jax....]
    all_gather x2 -> x0, blocking collectives: 65.6 us -> none  [the longest x1 40.4 us: per_device(): lax.all_gather(summed, 'dp', axis=0, tiled=True).astype(jnp.float32)]
    all_to_all x1 -> x0, blocking collectives: 31.6 us -> none  [per_device(): lax.all_to_all(local_grad.reshape(copies, part_rows, model_width), 'dp',...]
    all_to_all x2 -> x0, waiting for transfers between devices: 26.6 us -> none  [the longest x1 14.9 us: per_device(): lax.all_to_all(outgoing.reshape(groups, capacity, model_width), 'table',...]
    all_to_all x2 -> x0, starting transfers between devices: 7.6 us -> none  [the longest x1 4.13 us: per_device(): lax.all_to_all(dense_part.reshape(groups, dense_rows, model_width), 'tabl...]
    reduce_sum x3 -> x0, other arithmetic: 3.24 us -> none  [the longest x1 1.73 us: per_device(): jnp.sum(dense_terms.astype(jnp.float32), axis=0).astype(jnp.bfloat16)]
  transfers between devices with their start and end apart: 4 -> 1, of which waited for: 3 -> 1; matrix products, arithmetic and copies ran while one was open for 4% -> 0% of each run, Pallas kernels for 0% -> 0%
where the time goes in v2:
time: 143 us; the launch traced here: 142 us
  Pallas kernels  66 us (46%)
  matrix products  19.3 us (13%)
  blocking collectives  18.6 us (13%)
  waiting for transfers between devices  16.6 us (12%)
  local copies, waits for them, and re-layouts  8.83 us (6%)
  other arithmetic  7.55 us (5%)
  starting transfers between devices  4.02 us (3%)
  between operations  1.51 us (1%)
    pallas_call x1, Pallas kernels, exchange(): pl.pallas_call(functools.partial(exchange_kernel, scale), out_shape=(jax....  66 us
    all_to_all x1, blocking collectives, per_device(): lax.all_to_all(requested, 'table', split_axis=0, concat_axis=0, tiled=True)  18.6 us
    all_to_all x1, waiting for transfers between devices, per_device(): lax.all_to_all(reply.reshape(groups, capacity, model_width), 'table', spl...  16.6 us
    dot_general x2, matrix products, hstu_layer(): jnp.dot(normed.reshape(samples_here * seq_span, model_width), w_in, prefe...  5.74 us
    dot_general x3, matrix products, hstu_layer(): jnp.einsum('bhlm,bmhd->blhd', weights.astype(jnp.float32), values.astype(...  4.35 us
    all_to_all x1, starting transfers between devices, per_device(): lax.all_to_all(reply.reshape(groups, capacity, model_width), 'table', spl...  4.02 us
    dot_general x3, matrix products, hstu_layer(): jnp.einsum('blhd,bmhd->bhlm', queries.astype(jnp.float32), keys.astype(jn...  3.55 us
  transfers between devices with their start and end apart: 1, of which 1 were waited for; matrix products, arithmetic and copies ran while one was open for 0% of the time, Pallas kernels for 0%

profile of v2, /device:TPU:1, one launch (start us, length us, event | category | flops | bytes accessed | tf_op | source)
XLA Modules:
  0.0 142.4 jit_solution(6402047274323797285)
XLA Ops:
  0.6 0.0 copy-start
  0.6 0.8 fusion.59
  1.5 0.6 reduce-window.6
  2.0 0.2 slice_reduce_fusion
  2.3 0.8 fusion.58
  3.1 0.7 multiply_add_fusion.2
  3.7 0.8 select_reduce_fusion
  4.6 0.1 all_to_all.9
  4.6 18.6 %all_to_all.14 = s32[16,1,32]{2,1,0:T(1,128)S(1)} all-to-all(s32[16,1,32]{2,1,0:T(1,128)S(1)} %all_to_all.9), channel_id=1, replica_groups=mesh['dp'=32,'table'=16] {'table'}, dimensions={0} | all-to-all | bytes 4096 | tf_op jit(solution)/shard_map/all_to_all | solution.py:414
  23.3 0.5 broadcast.201
  23.8 0.7 reduce.19
  24.5 0.1 eq.61
  24.6 2.5 %fusion.15 = bf16[512,512]{1,0:T(8,128)(2,1)} fusion(bf16[768,512]{1,0:T(8,128)(2,1)} %param.7, s32[512]{0:T(512)S(1)} %eq.61), kind=kOutput, calls=%fused_computation.20 | convolution fusion | flops 403308544 | bytes 1312768 | tf_op jit(solution)/shard_map/dot_general | solution.py:417
  27.1 4.0 %all-to-all-start.1 = ((bf16[16,32,512]{2,1,0:T(8,128)(2,1)}), bf16[16,32,512]{2,1,0:T(8,128)(2,1)S(1)}, u32[]{:S(2)}, u32[]{:S(2)}) async-start(bf16[16,32,512]{2,1,0:T(8,128)(2,1)} %bitcast.6), calls=%async_computation.1 | async-start | bytes 1048576 | tf_op jit(solution)/shard_map/all_to_all | solution.py:420
  31.8 0.1 reshape_reshape.3.incoming
  31.9 16.6 %all-to-all-done.1 = bf16[16,32,512]{2,1,0:T(8,128)(2,1)S(1)} async-done(((bf16[16,32,512]{2,1,0:T(8,128)(2,1)}), bf16[16,32,512]{2,1,0:T(8,128)(2,1)S(1)}, u32[]{:S(2)}, u32[]{:S(2)}) %all-to-all-start.1) | async-done | bytes 524320 | tf_op jit(solution)/shard_map/all_to_all | solution.py:420
  48.5 0.4 fusion.69
  48.9 0.2 multiply_reduce_fusion.2
  49.1 2.7 %fusion.67 = (bf16[256,2048]{1,0:T(8,128)(2,1)S(1)}, f32[256,2048]{1,0:T(8,128)}, f32[256,2048]{1,0:T(8,128)}) fusion(bf16[512,2048]{1,0:T(8,128)(2,1)S(1)} %copy-done, f32[256,512]{1,0:T(8,128)S(1)} %get-tuple-element.19, f32[256]{0:T(256)S(1)} %fusion.60, f32[256]{0:T(256)S(1)} %broadcast_multiply_fusion.1), kind=kOutput, calls=%fused_computation.108 | convolution fusion | flops 539885568 | bytes 7866368 | tf_op jit(solution)/shard_map/jvp()/dot_general | solution.py:29
  51.9 0.1 slice_bitcast_fusion
  51.9 0.1 copy.67
  52.1 0.1 copy.66
  52.2 0.5 copy-done.6
  52.8 1.6 %divide_convert_fusion = (bf16[4,256,256]{2,1,0:T(8,128)(2,1)S(1)}, f32[4,256,256]{2,1,0:T(8,128)}) fusion(f32[]{:T(128)} %bitcast.8, pred[256,256]{1,0:T(8,128)(4,1)S(1)} %fusion.53, bf16[256,4,128]{0,2,1:T(8,128)(2,1)S(1)} %bitcast.103, bf16[256,4,128]{0,2,1:T(8,128)(2,1)S(1)} %bitcast.101), kind=kOutput, calls=%fused_computation.41 | convolution fusion | flops 69206016 | bytes 2162692 | tf_op jit(solution)/shard_map/jvp(blhd,bmhd->bhlm)/dot_general | solution.py:40
  54.4 0.3 fusion.70
  54.7 0.1 fusion.36
  54.8 0.3 copy-done.4
  55.2 0.2 copy.61
  55.4 0.1 copy-done.3
  55.5 1.8 %multiply_reduce_fusion.1 = (f32[256]{0:T(256)S(1)}, f32[256,512]{1,0:T(8,128)S(1)}) fusion(f32[256,512]{1,0:T(8,128)S(1)} %copy.61, f32[256]{0:T(256)S(1)} %broadcast_multiply_fusion, f32[256,2048]{1,0:T(8,128)} %get-tuple-element.11, bf16[512,512]{1,0:T(8,128)(2,1)} %param.12, bf16[1,256,512]{2,1,0:T(8,128)(2,1)S(1)} %copy-done.3, ...), kind=kOutput, calls=%fused_computation.53 | convolution fusion | flops 135134976 | bytes 2361600 | tf_op jit(solution)/shard_map/transpose(jvp())/dot_general | solution.py:56
  57.3 0.0 copy-done.5
  57.3 0.5 convolution_convert_fusion.1
  57.8 1.0 fusion.66
  58.8 0.1 broadcast_add_fusion
  58.9 0.1 copy.62
  59.0 2.0 %fusion.73 = bf16[4,128,256]{2,1,0:T(8,128)(2,1)} fusion(bf16[4,128,256]{2,1,0:T(8,128)(2,1)S(1)} %bitcast.106, bf16[4,256,256]{2,1,0:T(8,128)(2,1)} %copy-done.4), kind=kOutput, calls=%fused_computation.113 | convolution fusion | flops 67108864 | bytes 1048576 | tf_op jit(solution)/shard_map/transpose(jvp(bhlm,bmhd->blhd))/dot_general | solution.py:52
  61.0 2.0 %fusion.29 = bf16[4,256,256]{2,1,0:T(8,128)(2,1)S(1)} fusion(f32[4,256,256]{2,1,0:T(8,128)} %get-tuple-element.22, bf16[4,128,256]{2,1,0:T(8,128)(2,1)S(1)} %bitcast.107, f32[]{:T(128)} %bitcast.8, pred[256,256]{1,0:T(8,128)(4,1)S(1)} %fusion.53, bf16[32,4,8,128]{3,2,1,0:T(8,128)(2,1)} %copy-done.10), kind=kOutput, calls=%fused_computation.37 | convolution fusion | flops 70778880 | bytes 2162692 | tf_op jit(solution)/shard_map/transpose(jvp(bhlm,bmhd->blhd))/dot_general | solution.py:52
  63.1 1.0 fusion.71
  64.1 1.0 fusion.72
  65.1 1.8 %copy.65 = bf16[256,512]{1,0:T(8,128)(2,1)} copy(bf16[256,512]{0,1:T(8,128)(2,1)} %bitcast.105) | data formatting | bytes 524288 | tf_op jit(solution)/shard_map/transpose(jvp())/convert_element_type | solution.py:37
  66.9 1.8 %copy.63 = bf16[256,512]{1,0:T(8,128)(2,1)} copy(bf16[256,512]{0,1:T(8,128)(2,1)} %bitcast.109) | data formatting | bytes 524288 | tf_op jit(solution)/shard_map/transpose(jvp())/convert_element_type | solution.py:39
  68.7 1.8 %copy.64 = bf16[256,512]{1,0:T(8,128)(2,1)} copy(bf16[256,512]{0,1:T(8,128)(2,1)} %bitcast.108) | data formatting | bytes 524288 | tf_op jit(solution)/shard_map/transpose(jvp())/convert_element_type | solution.py:38
  70.5 3.0 %multiply_reduce_fusion = (f32[256]{0:T(256)S(1)}, f32[256,512]{1,0:T(8,128)S(1)}) fusion(f32[256,512]{1,0:T(8,128)S(1)} %copy-done.2, f32[256]{0:T(256)S(1)} %broadcast_multiply_fusion.1, bf16[512,2048]{1,0:T(8,128)(2,1)S(1)} %copy-done, f32[256,2048]{1,0:T(8,128)} %get-tuple-element.20, f32[256,512]{1,0:T(8,128)} %get-tuple-element.12, ...), kind=kOutput, calls=%fused_computation.52 | convolution fusion | flops 545390336 | bytes 6555648 | tf_op jit(solution)/shard_map/transpose(jvp())/dot_general | solution.py:29
  73.5 0.3 fusion.65
  73.8 0.5 convolution_convert_fusion.2
  74.3 66.0 %shard_map.86 = (bf16[768,512]{1,0:T(8,128)(2,1)S(1)}, bf16[512,512]{1,0:T(8,128)(2,1)S(1)}) custom-call(bf16[16,32,512]{2,1,0:T(8,128)(2,1)S(1)} %bitcast.98, bf16[16,32,512]{2,1,0:T(8,128)(2,1)S(1)} %bitcast.97, s32[1,512]{1,0:T(1,128)S(1)} %reshape_reshape.3.incoming), custom_call_target="tpu_custom_call" | custom-call | tf_op jit(solution)/shard_map/pallas_call | solution.py:360
  140.3 1.4 convert_element_type.151
  141.6 0.8 copy.83
  (28 shorter events, 0.2 us)
Async XLA Ops:
  0.6 48.5 %copy-start = (bf16[512,2048]{1,0:T(8,128)(2,1)S(1)}, bf16[512,2048]{1,0:T(8,128)(2,1)}, u32[]{:S(2)}) copy-start(bf16[512,2048]{1,0:T(8,128)(2,1)} %param.11) | copy-start | bytes 6291460
  27.1 21.4 %all-to-all-start.1 = ((bf16[16,32,512]{2,1,0:T(8,128)(2,1)}), bf16[16,32,512]{2,1,0:T(8,128)(2,1)S(1)}, u32[]{:S(2)}, u32[]{:S(2)}) async-start(bf16[16,32,512]{2,1,0:T(8,128)(2,1)} %bitcast.6), calls=%async_computation.1 | async-start | bytes 1048576 | tf_op jit(solution)/shard_map/all_to_all | solution.py:420
  48.9 3.0 %copy-start.1 = (f32[256,512]{1,0:T(8,128)}, f32[256,512]{1,0:T(8,128)S(1)}, u32[]{:S(2)}) copy-start(f32[256,512]{1,0:T(8,128)S(1)} %get-tuple-element.19) | copy-start | bytes 1572868
  51.9 2.4 %copy-start.10 = (bf16[32,4,8,128]{3,2,1,0:T(8,128)(2,1)}, bf16[32,4,8,128]{3,2,1,0:T(8,128)(2,1)S(1)}, u32[]{:S(2)}) copy-start(bf16[32,4,8,128]{3,2,1,0:T(8,128)(2,1)S(1)} %get-tuple-element.13) | copy-start | bytes 786436
  52.1 0.7 copy-start.6
  52.2 2.1 %copy-start.8 = (bf16[256,512]{0,1:T(8,128)(2,1)}, bf16[256,512]{0,1:T(8,128)(2,1)S(1)}, u32[]{:S(2)}) copy-start(bf16[256,512]{0,1:T(8,128)(2,1)S(1)} %copy.66) | copy-start | bytes 786436
  54.4 0.8 copy-start.4
  54.4 1.1 copy-start.3
  55.4 1.9 %copy-start.5 = (f32[256,2048]{1,0:T(8,128)S(1)}, f32[256,2048]{1,0:T(8,128)}, u32[]{:S(2)}) copy-start(f32[256,2048]{1,0:T(8,128)} %get-tuple-element.11) | copy-start | bytes 6291460
  61.0 2.0 %copy-start.7 = (bf16[256,512]{0,1:T(8,128)(2,1)S(1)}, bf16[256,512]{0,1:T(8,128)(2,1)}, u32[]{:S(2)}) copy-start(bf16[256,512]{0,1:T(8,128)(2,1)} %copy-done.6) | copy-start | bytes 786436
  61.0 3.1 %copy-start.9 = (bf16[256,512]{0,1:T(8,128)(2,1)S(1)}, bf16[256,512]{0,1:T(8,128)(2,1)}, u32[]{:S(2)}) copy-start(bf16[256,512]{0,1:T(8,128)(2,1)} %copy-done.8) | copy-start | bytes 786436
  63.1 7.4 %copy-start.2 = (f32[256,512]{1,0:T(8,128)S(1)}, f32[256,512]{1,0:T(8,128)}, u32[]{:S(2)}) copy-start(f32[256,512]{1,0:T(8,128)} %copy-done.1) | copy-start | bytes 1572868

commit v3 on v2

--- a/solution.py
+++ b/solution.py
@@ -57,10 +57,6 @@
         -1, model_width
     ).astype(jnp.float32)
     return (output, mixed)
-
-
-def pick_rows(index, length):
-    return (index[:, None] == jnp.arange(length, dtype=jnp.int32)[None, :]).astype(jnp.bfloat16)
 
 
 def send(src, dst, send_sem, recv_sem, **where):
@@ -170,10 +166,10 @@
         send(dense_part.at[p], dense_arr.at[p], dz_s.at[p], dz_r.at[p], table=p).wait_recv()
 
     each(1, nz, lambda k: z_copy(zp(k)).start())
-    each(1, nz, lambda k: dz_copy(zp(k)).start())
     arrived[me] = outgoing[me]
     dense_arr[me] = dense_part[me]
     each(1, nz, lambda k: z_wait(zp(k)))
+    each(1, nz, lambda k: dz_copy(zp(k)).start())
 
     def x_copy(p, c):
         return send(part.at[p, c], x_in.at[x, c], x_s.at[p, c], x_r.at[x, c], dp=at_x(p))
@@ -395,6 +391,137 @@
     )(outgoing, dense_part, incoming)
 
 
+def dot_first(a, b):
+    return lax.dot_general(a, b, (((0,), (0,)), ((), ())), preferred_element_type=jnp.float32)
+
+
+def hot(shape, index):
+    line = lax.broadcasted_iota(jnp.int32, shape, 0)
+    return (line == index).astype(jnp.float32).astype(jnp.bfloat16)
+
+
+def fetch_kernel(
+    table,
+    owners,
+    rows,
+    embedded,
+    position,
+    incoming,
+    req_out,
+    req_in,
+    reply,
+    got,
+    q_s,
+    q_r,
+    r_s,
+    r_r,
+):
+    nz, cap, width = got.shape
+    slots = owners.shape[1]
+    shard_rows = table.shape[0]
+    per = 128 // cap
+    me = lax.axis_index("table")
+    f32, bf16 = jnp.float32, jnp.bfloat16
+
+    def zp(k):
+        return lax.rem(me + k, nz)
+
+    barrier = pltpu.get_barrier_semaphore()
+    each(
+        1,
+        nz,
+        lambda k: pl.semaphore_signal(
+            barrier, inc=1, device_id={"table": zp(k)}, device_id_type=MESH
+        ),
+    )
+    own = owners[...]
+    hits = (lax.broadcasted_iota(jnp.int32, (nz, slots), 0) == own).astype(f32)
+    earlier = (
+        lax.broadcasted_iota(jnp.int32, (slots, slots), 0)
+        < lax.broadcasted_iota(jnp.int32, (slots, slots), 1)
+    ).astype(f32)
+    ahead = jnp.dot(hits.astype(bf16), earlier.astype(bf16), preferred_element_type=f32)
+    rank = jnp.sum(hits * ahead, axis=0, keepdims=True).astype(jnp.int32)
+    place = own * cap + rank
+    position[...] = place
+    pick = hot((nz * 128, slots), own * 128 + lax.rem(me, per) * cap + rank)
+    wanted = rows[...]
+    high = lax.shift_right_logical(wanted, 8)
+    low = wanted & 255
+    which = lax.broadcasted_iota(jnp.int32, (8, slots), 0)
+    both = jnp.where(which == 0, high, jnp.where(which == 1, low, 0)).astype(f32).astype(bf16)
+    found = lax.dot_general(both, pick, (((1,), (1,)), ((), ())), preferred_element_type=f32)
+    asked = (found[0:1] * 256.0 + found[1:2]).astype(jnp.int32)
+    for p in range(nz):
+        req_out[p] = asked[:, p * 128 : (p + 1) * 128]
+    pl.semaphore_wait(barrier, nz - 1)
+
+    def q_copy(p):
+        return send(req_out.at[p], req_in.at[me], q_s.at[p], q_r.at[me], table=p)
+
+    def q_wait(p):
+        send(req_out.at[p], req_in.at[p], q_s.at[p], q_r.at[p], table=p).wait_recv()
+
+    def r_copy(p):
+        return send(reply.at[p], got.at[me], r_s.at[p], r_r.at[me], table=p)
+
+    def r_wait(p):
+        send(reply.at[p], got.at[p], r_s.at[p], r_r.at[p], table=p).wait_recv()
+
+    each(1, nz, lambda k: q_copy(zp(k)).start())
+    req_in[me] = req_out[me]
+    each(1, nz, lambda k: q_wait(zp(k)))
+    for g in range(nz // per):
+        line = req_in[g * per]
+        for j in range(1, per):
+            line = line + req_in[g * per + j]
+        incoming[:, g * 128 : (g + 1) * 128] = line
+        block = dot_first(hot((shard_rows, 128), line), table[...]).astype(bf16)
+        for j in range(per):
+            reply[g * per + j] = block[j * cap : (j + 1) * cap]
+    each(1, nz, lambda k: r_copy(zp(k)).start())
+    got[me] = reply[me]
+    each(1, nz, lambda k: r_wait(zp(k)))
+    spread = hot((nz * cap, slots), place)
+    embedded[...] = dot_first(spread, got[...].reshape(nz * cap, width)).astype(bf16)
+
+    def sent(k):
+        q_copy(zp(k)).wait_send()
+        r_copy(zp(k)).wait_send()
+
+    each(1, nz, sent)
+
+
+def fetch(table, owners, rows, groups, capacity):
+    shard_rows, width = table.shape
+    slots = owners.shape[1]
+    vmem = pl.BlockSpec(memory_space=pltpu.VMEM)
+    dma = pltpu.SemaphoreType.DMA
+    return pl.pallas_call(
+        fetch_kernel,
+        out_shape=(
+            jax.ShapeDtypeStruct((slots, width), jnp.bfloat16),
+            jax.ShapeDtypeStruct((1, slots), jnp.int32),
+            jax.ShapeDtypeStruct((1, groups * capacity), jnp.int32),
+        ),
+        in_specs=[vmem] * 3,
+        out_specs=(vmem, vmem, vmem),
+        scratch_shapes=[
+            pltpu.VMEM((groups, 1, 128), jnp.int32),
+            pltpu.VMEM((groups, 1, 128), jnp.int32),
+            pltpu.VMEM((groups, capacity, width), jnp.bfloat16),
+            pltpu.VMEM((groups, capacity, width), jnp.bfloat16),
+            dma((groups,)),
+            dma((groups,)),
+            dma((groups,)),
+            dma((groups,)),
+        ],
+        compiler_params=pltpu.CompilerParams(
+            collective_id=1, has_side_effects=True, vmem_limit_bytes=32 << 20
+        ),
+    )(table, owners, rows)
+
+
 def per_device(table, history_shard, history_row, lengths, w_in, w_out, cotangent):
     shard_rows, model_width = table.shape
     samples_here, seq_span = history_row.shape
@@ -402,26 +529,15 @@
     copies = lax.axis_size("dp")
     slot_count = samples_here * seq_span
     capacity = 2 * slot_count // groups
-    owners = history_shard[:, :, 0].reshape(-1)
-    local_rows = history_row.reshape(-1)
-    owner_hits = (owners[:, None] == jnp.arange(groups)[None, :]).astype(jnp.int32)
-    slot_rank = jnp.sum((jnp.cumsum(owner_hits, axis=0) - owner_hits) * owner_hits, axis=1)
-    position = owners * capacity + slot_rank
-    slot_hits = position[:, None] == jnp.arange(groups * capacity, dtype=jnp.int32)[None, :]
-    requested = jnp.sum(jnp.where(slot_hits, local_rows[:, None], 0), axis=0).reshape(
-        groups, capacity
-    )
-    incoming = lax.all_to_all(requested, "table", split_axis=0, concat_axis=0, tiled=True).reshape(
-        -1
-    )
-    reply = jnp.dot(
-        pick_rows(incoming, shard_rows), table, preferred_element_type=jnp.float32
-    ).astype(jnp.bfloat16)
-    received = lax.all_to_all(
-        reply.reshape(groups, capacity, model_width), "table", split_axis=0, concat_axis=0, tiled=True
-    ).reshape(groups * capacity, model_width)
-    place = slot_hits.astype(jnp.bfloat16)
-    embedded = jnp.dot(place, received, preferred_element_type=jnp.float32).astype(jnp.bfloat16)
+    embedded, position, incoming = fetch(
+        table,
+        history_shard.reshape(1, slot_count),
+        history_row.reshape(1, slot_count),
+        groups,
+        capacity,
+    )
+    slots_at = jnp.arange(groups * capacity, dtype=jnp.int32)[:, None]
+    place = (slots_at == position).astype(jnp.bfloat16)
     embedded = embedded.reshape(samples_here, seq_span, model_width)
     output, pullback, mixed = jax.vjp(
         lambda rows_in: hstu_layer(rows_in, w_in, w_out, lengths), embedded, has_aux=True
@@ -436,16 +552,13 @@
         mixed, flat_seed, (((0,), (0,)), ((), ())), preferred_element_type=jnp.float32
     ).astype(jnp.bfloat16)
     (row_grad,) = pullback(flat_seed.astype(jnp.float32))
-    outgoing = lax.dot_general(
-        place,
-        row_grad.reshape(-1, model_width),
-        (((0,), (0,)), ((), ())),
-        preferred_element_type=jnp.float32,
+    outgoing = jnp.dot(
+        place, row_grad.reshape(-1, model_width), preferred_element_type=jnp.float32
     ).astype(jnp.bfloat16)
     table_sum, dense_grad = exchange(
         outgoing.reshape(groups, capacity, model_width),
         dense_part.reshape(groups, capacity, model_width),
-        incoming.reshape(1, groups * capacity),
+        incoming,
         shard_rows,
         grad_scale,
     )

time: 143 us -> 128 us (0.90)
  Pallas kernels: 66 us -> 96.5 us
  blocking collectives: 18.6 us -> 0 us
  waiting for transfers between devices: 16.6 us -> 0 us
  other arithmetic: 7.55 us -> 3.29 us
  starting transfers between devices: 4.02 us -> 0 us
  matrix products: 19.3 us -> 17.3 us
    pallas_call x0 -> x1, Pallas kernels: none -> 30.8 us  [fetch(): pl.pallas_call(fetch_kernel, out_shape=(jax.ShapeDtypeStruct((slots, widt...]
    all_to_all x1 -> x0, blocking collectives: 18.6 us -> none  [per_device(): lax.all_to_all(requested, 'table', split_axis=0, concat_axis=0, tiled=True)]
    all_to_all x1 -> x0, waiting for transfers between devices: 16.6 us -> none  [per_device(): lax.all_to_all(reply.reshape(groups, capacity, model_width), 'table', spl...]
    all_to_all x1 -> x0, starting transfers between devices: 4.02 us -> none  [per_device(): lax.all_to_all(reply.reshape(groups, capacity, model_width), 'table', spl...]
    dot_general x3 -> x1, matrix products: 3.46 us -> 0.54 us  [per_device(): jnp.dot(place, row_grad.reshape(-1, model_width), preferred_element_type=...]
    unnamed x24 -> x28, local copies, waits for them, and re-layouts: 1.89 us -> 3.88 us
    dot_general x3, matrix products: 3.55 us -> 5.44 us  [hstu_layer(): jnp.einsum('blhd,bmhd->bhlm', queries.astype(jnp.float32), keys.astype(jn...]
    reduce_sum x2 -> x1, other arithmetic: 1.6 us -> 0.11 us  [layer_norm(): average = jnp.mean(values, axis=-1, keepdims=True)]
  transfers between devices with their start and end apart: 1 -> 0, of which waited for: 1 -> 0; matrix products, arithmetic and copies ran while one was open for 0% -> 0% of each run, Pallas kernels for 0% -> 0%
where the time goes in v3:
time: 128 us
  Pallas kernels  96.5 us (75%)
  matrix products  17.3 us (14%)
  local copies, waits for them, and re-layouts  9.21 us (7%)
  other arithmetic  3.29 us (3%)
  between operations  1.67 us (1%)
    pallas_call x1, Pallas kernels, exchange(): pl.pallas_call(functools.partial(exchange_kernel, scale), out_shape=(jax....  65.7 us
    pallas_call x1, Pallas kernels, fetch(): pl.pallas_call(fetch_kernel, out_shape=(jax.ShapeDtypeStruct((slots, widt...  30.8 us
    dot_general x2, matrix products, hstu_layer(): jnp.dot(normed.reshape(samples_here * seq_span, model_width), w_in, prefe...  5.64 us
    dot_general x3, matrix products, hstu_layer(): jnp.einsum('blhd,bmhd->bhlm', queries.astype(jnp.float32), keys.astype(jn...  5.44 us
    unnamed x28, local copies, waits for them, and re-layouts  3.88 us
    dot_general x3, matrix products, hstu_layer(): jnp.einsum('bhlm,bmhd->blhd', weights.astype(jnp.float32), values.astype(...  3.4 us

profile of v3, /device:TPU:1, one launch (start us, length us, event | category | flops | bytes accessed | tf_op | source)
XLA Modules:
  0.0 128.1 jit_solution(958183666944918022)
XLA Ops:
  0.6 0.0 copy-start
  1.5 0.0 copy-start.1
  1.5 1.1 copy-done.1
  2.6 0.7 copy-done.2
  3.3 0.7 copy-done.3
  4.0 30.8 %shard_map.86 = (bf16[256,512]{1,0:T(8,128)(2,1)S(1)}, s32[1,256]{1,0:T(1,128)S(1)}, s32[1,512]{1,0:T(1,128)S(1)}) custom-call(bf16[768,512]{1,0:T(8,128)(2,1)S(1)} %copy-done.1, s32[1,256]{1,0:T(1,128)S(1)} %bitcast.74, s32[1,256]{1,0:T(1,128)S(1)} %copy-done.3), custom_call_target="tpu_custom_call" | custom-call | tf_op jit(solution)/shard_map/pallas_call | solution.py:500
  34.8 0.1 convert_reduce_fusion
  35.0 0.2 fusion.35
  35.2 0.0 copy-done
  35.2 2.7 %fusion.66 = (bf16[256,2048]{1,0:T(8,128)(2,1)S(1)}, f32[256,2048]{1,0:T(8,128)}, f32[256,2048]{1,0:T(8,128)}) fusion(bf16[512,2048]{1,0:T(8,128)(2,1)S(1)} %copy-done, bf16[256,512]{1,0:T(8,128)(2,1)S(1)} %get-tuple-element.8, f32[256]{0:T(256)S(1)} %fusion.59, f32[256]{0:T(256)S(1)} %broadcast_multiply_fusion.1), kind=kOutput, calls=%fused_computation.96 | convolution fusion | flops 540016640 | bytes 7604224 | tf_op jit(solution)/shard_map/jvp()/dot_general | solution.py:29
  37.9 0.1 slice_bitcast_fusion
  38.0 0.0 copy-start.12
  38.0 0.1 copy.28
  38.1 0.0 copy-start.9
  38.1 0.1 copy.27
  38.3 0.0 copy-start.10
  38.3 1.6 %divide_convert_fusion = (bf16[4,256,256]{2,1,0:T(8,128)(2,1)S(1)}, f32[4,256,256]{2,1,0:T(8,128)}) fusion(f32[]{:T(128)} %bitcast.4, pred[256,256]{1,0:T(8,128)(4,1)S(1)} %fusion.56, bf16[256,4,128]{0,2,1:T(8,128)(2,1)S(1)} %bitcast.79, bf16[256,4,128]{0,2,1:T(8,128)(2,1)S(1)} %bitcast.77), kind=kOutput, calls=%fused_computation.36 | convolution fusion | flops 69206016 | bytes 2162692 | tf_op jit(solution)/shard_map/jvp(blhd,bmhd->bhlm)/dot_general | solution.py:40
  39.9 0.0 copy-done.9
  39.9 0.0 copy-done.10
  39.9 0.0 copy-done.12
  39.9 0.3 fusion.68
  40.2 0.4 copy-done.4
  40.7 0.1 fusion.39
  40.8 0.2 copy.22
  41.0 0.0 copy-start.6
  41.0 0.0 copy-start.7
  41.0 1.9 %multiply_reduce_fusion = (f32[256]{0:T(256)S(1)}, f32[256,512]{1,0:T(8,128)S(1)}) fusion(f32[256,512]{1,0:T(8,128)S(1)} %copy.22, f32[256]{0:T(256)S(1)} %broadcast_multiply_fusion, f32[256,2048]{1,0:T(8,128)} %get-tuple-element.15, bf16[512,512]{1,0:T(8,128)(2,1)} %param.12, bf16[1,256,512]{2,1,0:T(8,128)(2,1)} %param.13, ...), kind=kOutput, calls=%fused_computation.55 | convolution fusion | flops 135134976 | bytes 2361600 | tf_op jit(solution)/shard_map/transpose(jvp())/dot_general | solution.py:56
  42.9 0.1 copy-done.6
  43.0 0.5 convolution_convert_fusion.1
  43.4 1.0 fusion.65
  44.5 0.1 broadcast_add_fusion
  44.6 0.9 copy.23
  45.4 2.1 %fusion.26 = bf16[4,256,256]{2,1,0:T(8,128)(2,1)S(1)} fusion(f32[4,256,256]{2,1,0:T(8,128)} %get-tuple-element.24, bf16[4,128,256]{2,1,0:T(8,128)(2,1)} %bitcast.81, f32[]{:T(128)} %bitcast.4, pred[256,256]{1,0:T(8,128)(4,1)S(1)} %fusion.56, bf16[32,4,8,128]{3,2,1,0:T(8,128)(2,1)} %copy-done.12), kind=kOutput, calls=%fused_computation.32 | convolution fusion | flops 70778880 | bytes 2162692 | tf_op jit(solution)/shard_map/transpose(jvp(bhlm,bmhd->blhd))/dot_general | solution.py:52
  47.6 0.0 copy-done.5
  47.6 0.0 copy-done.11
  47.6 0.9 fusion.71
  48.5 1.8 %copy.26 = bf16[256,512]{1,0:T(8,128)(2,1)} copy(bf16[256,512]{0,1:T(8,128)(2,1)} %bitcast.84) | data formatting | bytes 524288 | tf_op jit(solution)/shard_map/transpose(jvp())/convert_element_type | solution.py:37
  50.3 2.0 %fusion.69 = bf16[4,256,128]{1,2,0:T(8,128)(2,1)} fusion(bf16[4,256,256]{2,1,0:T(8,128)(2,1)S(1)} %fusion.26, bf16[256,4,128]{0,2,1:T(8,128)(2,1)} %bitcast.78), kind=kOutput, calls=%fused_computation.98 | convolution fusion | flops 67108864 | bytes 1048576 | tf_op jit(solution)/shard_map/transpose(jvp(blhd,bmhd->bhlm))/dot_general | solution.py:40
  52.3 1.9 %fusion.70 = bf16[4,256,128]{1,2,0:T(8,128)(2,1)} fusion(bf16[4,256,256]{2,1,0:T(8,128)(2,1)S(1)} %fusion.26, bf16[256,4,128]{0,2,1:T(8,128)(2,1)} %bitcast.80), kind=kOutput, calls=%fused_computation.99 | convolution fusion | flops 67108864 | bytes 1048576 | tf_op jit(solution)/shard_map/transpose(jvp(blhd,bmhd->bhlm))/dot_general | solution.py:40
  54.2 1.1 copy.24
  55.3 1.1 copy.25
  56.4 0.0 copy-start.8
  56.4 2.9 %fusion.37 = (f32[256]{0:T(256)S(1)}, f32[256,512]{1,0:T(8,128)S(1)}) fusion(bf16[256,512]{1,0:T(8,128)(2,1)S(1)} %get-tuple-element.8, f32[256]{0:T(256)S(1)} %broadcast_multiply_fusion.1, bf16[512,2048]{1,0:T(8,128)(2,1)S(1)} %copy-done, f32[256,2048]{1,0:T(8,128)} %get-tuple-element.22, f32[256,512]{1,0:T(8,128)} %get-tuple-element.16, ...), kind=kOutput, calls=%fused_computation.49 | convolution fusion | flops 545521408 | bytes 6293504 | tf_op jit(solution)/shard_map/transpose(jvp())/dot_general | solution.py:29
  59.3 0.3 fusion.64
  59.6 0.5 convolution_convert_fusion.2
  60.2 65.7 %shard_map.87 = (bf16[768,512]{1,0:T(8,128)(2,1)S(1)}, bf16[512,512]{1,0:T(8,128)(2,1)S(1)}) custom-call(bf16[16,32,512]{2,1,0:T(8,128)(2,1)S(1)} %bitcast.73, bf16[16,32,512]{2,1,0:T(8,128)(2,1)S(1)} %bitcast.72, s32[1,512]{1,0:T(1,128)S(1)} %get-tuple-element.9.incoming), custom_call_target="tpu_custom_call" | custom-call | tf_op jit(solution)/shard_map/pallas_call | solution.py:356
  125.9 1.4 %convert_element_type.133 = f32[768,512]{1,0:T(8,128)} convert(bf16[768,512]{1,0:T(8,128)(2,1)S(1)} %get-tuple-element.10) | non-fusion elementwise | flops 393216 | bytes 2359296 | tf_op jit(solution)/shard_map/convert_element_type | solution.py:565
  127.3 0.8 copy.42
  (16 shorter events, 0.1 us)
Async XLA Ops:
  0.6 34.5 %copy-start = (bf16[512,2048]{1,0:T(8,128)(2,1)S(1)}, bf16[512,2048]{1,0:T(8,128)(2,1)}, u32[]{:S(2)}) copy-start(bf16[512,2048]{1,0:T(8,128)(2,1)} %param.11) | copy-start | bytes 6291460
  1.5 1.1 copy-start.1
  2.6 0.7 copy-start.2
  3.3 0.7 copy-start.3
  38.0 1.9 %copy-start.12 = (bf16[32,4,8,128]{3,2,1,0:T(8,128)(2,1)}, bf16[32,4,8,128]{3,2,1,0:T(8,128)(2,1)S(1)}, u32[]{:S(2)}) copy-start(bf16[32,4,8,128]{3,2,1,0:T(8,128)(2,1)S(1)} %get-tuple-element.17) | copy-start | bytes 786436
  38.1 1.7 %copy-start.9 = (bf16[256,512]{0,1:T(8,128)(2,1)}, bf16[256,512]{0,1:T(8,128)(2,1)S(1)}, u32[]{:S(2)}) copy-start(bf16[256,512]{0,1:T(8,128)(2,1)S(1)} %copy.28) | copy-start | bytes 786436
  38.3 1.6 %copy-start.10 = (bf16[256,512]{0,1:T(8,128)(2,1)}, bf16[256,512]{0,1:T(8,128)(2,1)S(1)}, u32[]{:S(2)}) copy-start(bf16[256,512]{0,1:T(8,128)(2,1)S(1)} %copy.27) | copy-start | bytes 786436
  39.9 0.8 copy-start.4
  41.0 2.0 %copy-start.6 = (f32[256,2048]{1,0:T(8,128)S(1)}, f32[256,2048]{1,0:T(8,128)}, u32[]{:S(2)}) copy-start(f32[256,2048]{1,0:T(8,128)} %get-tuple-element.15) | copy-start | bytes 6291460
  41.0 2.0 %copy-start.7 = (bf16[1,256,512]{2,1,0:T(8,128)(2,1)S(1)}, bf16[1,256,512]{2,1,0:T(8,128)(2,1)}, u32[]{:S(2)}) copy-start(bf16[1,256,512]{2,1,0:T(8,128)(2,1)} %param.13) | copy-start | bytes 786436
  45.4 2.1 %copy-start.5 = (bf16[4,256,256]{2,1,0:T(8,128)(2,1)S(1)}, bf16[4,256,256]{2,1,0:T(8,128)(2,1)}, u32[]{:S(2)}) copy-start(bf16[4,256,256]{2,1,0:T(8,128)(2,1)} %copy-done.4) | copy-start | bytes 1572868
  45.4 2.1 %copy-start.11 = (bf16[256,512]{0,1:T(8,128)(2,1)S(1)}, bf16[256,512]{0,1:T(8,128)(2,1)}, u32[]{:S(2)}) copy-start(bf16[256,512]{0,1:T(8,128)(2,1)} %copy.23) | copy-start | bytes 786436
  56.4 3.2 %copy-start.8 = (bf16[1,256,512]{2,1,0:T(8,128)(2,1)S(1)}, bf16[1,256,512]{2,1,0:T(8,128)(2,1)}, u32[]{:S(2)}) copy-start(bf16[1,256,512]{2,1,0:T(8,128)(2,1)} %param.13) | copy-start | bytes 786436

commit v4 on v3

--- a/solution.py
+++ b/solution.py
@@ -117,6 +117,12 @@
     dgx_r,
     dgz_s,
     dgz_r,
+    ds_s,
+    ds_r,
+    side_s,
+    x_mid,
+    d_side,
+    d_pair,
 ):
     nz, cap, width = outgoing.shape
     rows = table_out.shape[0]
@@ -137,6 +143,20 @@
     def yp(k):
         return lax.rem(y + k, NY)
 
+    side = me + 1 - 2 * lax.rem(me, 2)
+    x1 = x + 1 - 2 * lax.rem(x, 2)
+    x2 = lax.rem(x + 2, NX)
+    x3 = NX - 1 - x
+
+    def first(c):
+        return x1 + lax.rem(c, 2) * (x3 - x1)
+
+    def second(c):
+        return x3 + lax.rem(c, 2) * (x1 - x3)
+
+    def core(k):
+        return lax.rem(me + 2 * k, nz)
+
     def at_x(px):
         return px * NY + y
 
@@ -159,23 +179,37 @@
     def z_wait(p):
         send(outgoing.at[p], arrived.at[p], z_s.at[p], z_r.at[p], table=p).wait_recv()
 
-    def dz_copy(p):
-        return send(dense_part.at[p], dense_arr.at[me], dz_s.at[p], dz_r.at[me], table=p)
-
-    def dz_wait(p):
-        send(dense_part.at[p], dense_arr.at[p], dz_s.at[p], dz_r.at[p], table=p).wait_recv()
+    def ds_copy(k):
+        p = lax.rem(side + 2 * k, nz)
+        return send(dense_part.at[p], d_side.at[k], ds_s.at[k], ds_r.at[k], table=side)
+
+    def dz_copy(k):
+        return send(d_pair.at[k], dense_arr.at[k], dz_s.at[k], dz_r.at[k], table=core(k))
 
     each(1, nz, lambda k: z_copy(zp(k)).start())
+    each(0, nz // 2, lambda k: ds_copy(k).start())
     arrived[me] = outgoing[me]
-    dense_arr[me] = dense_part[me]
+
+    def pair_up(k):
+        ds_copy(k).wait_recv()
+        mine = dense_part[core(k)].astype(f32) + d_side[k].astype(f32)
+        d_pair[k] = mine.astype(bf16)
+
+    each(0, nz // 2, pair_up)
     each(1, nz, lambda k: z_wait(zp(k)))
-    each(1, nz, lambda k: dz_copy(zp(k)).start())
-
-    def x_copy(p, c):
-        return send(part.at[p, c], x_in.at[x, c], x_s.at[p, c], x_r.at[x, c], dp=at_x(p))
-
-    def x_wait(p, c):
-        send(part.at[p, c], x_in.at[p, c], x_s.at[p, c], x_r.at[p, c], dp=at_x(p)).wait_recv()
+    each(1, nz // 2, lambda k: dz_copy(k).start())
+
+    def xa_copy(c):
+        p = first(c)
+        return send(part.at[p, c], x_in.at[0, c], x_s.at[0, c], x_r.at[0, c], dp=at_x(p))
+
+    def xb_copy(c):
+        p = first(c)
+        return send(part.at[x2, c], x_in.at[1, c], x_s.at[1, c], x_r.at[1, c], dp=at_x(p))
+
+    def xc_copy(c):
+        p = second(c)
+        return send(x_mid.at[c], x_in.at[2, c], x_s.at[2, c], x_r.at[2, c], dp=at_x(p))
 
     def make_part(p):
         line = lax.broadcasted_iota(jnp.int32, (x_rows, nz * cap), 0) + p * x_rows
@@ -187,13 +221,24 @@
                 (c % 2) * half : (c % 2 + 1) * half, (c // 2) * 128 : (c // 2 + 1) * 128
             ]
 
-    def x_stage(k):
-        p = xp(k)
-        make_part(p)
-        each(1, NY + 1, lambda j: x_copy(p, yp(j)).start())
-
-    each(1, NX, x_stage)
+    def x_start(c):
+        xb_copy(c).start()
+        xa_copy(c).start()
+
+    def x_middle(c):
+        xb_copy(c).wait_recv()
+        held = part[second(c), c].astype(f32) + x_in[1, c].astype(f32)
+        x_mid[c] = held.astype(bf16)
+        xc_copy(c).start()
+
+    make_part(x2)
+    make_part(x1)
+    each(0, NY // 2, lambda i: x_start(2 * lax.rem(y // 2 + 1 + i, NY // 2)))
+    make_part(x3)
+    each(0, NY // 2, lambda i: x_start(2 * lax.rem(y // 2 + 1 + i, NY // 2) + 1))
     make_part(x)
+    each(0, NY // 2, lambda i: x_middle(2 * lax.rem(y // 2 + 1 + i, NY // 2)))
+    each(0, NY // 2, lambda i: x_middle(2 * lax.rem(y // 2 + 1 + i, NY // 2) + 1))
 
     def y_copy(c):
         return send(x_sum.at[c], y_in.at[y], y_s.at[c], y_r.at[y], dp=at_y(c))
@@ -202,11 +247,9 @@
         send(x_sum.at[c], y_in.at[c], y_s.at[c], y_r.at[c], dp=at_y(c)).wait_recv()
 
     def sum_x(c):
-        total = part[x, c].astype(f32)
-        for k in range(1, NX):
-            p = xp(k)
-            x_wait(p, c)
-            total = total + x_in[p, c].astype(f32)
+        xa_copy(c).wait_recv()
+        xc_copy(c).wait_recv()
+        total = part[x, c].astype(f32) + x_in[0, c].astype(f32) + x_in[2, c].astype(f32)
         x_sum[c] = total.astype(bf16)
 
     def y_stage(j):
@@ -223,9 +266,9 @@
     def dx_wait(p):
         send(dx_out.at[p], dx_in.at[p], dx_s.at[p], dx_r.at[p], dp=at_x(p)).wait_recv()
 
-    each(1, nz, lambda k: dz_wait(zp(k)))
-    dense_sum = dense_arr[0].astype(f32)
-    for k in range(1, nz):
+    each(1, nz // 2, lambda k: dz_copy(k).wait_recv())
+    dense_sum = d_pair[0].astype(f32)
+    for k in range(1, nz // 2):
         dense_sum = dense_sum + dense_arr[k].astype(f32)
     dense_sum = dense_sum.astype(bf16)
     for c in range(NX):
@@ -251,8 +294,17 @@
     def gx_wait(p, c):
         send(whole.at[p, c], whole.at[p, c], gx_s.at[p, c], gx_r.at[p, c], dp=at_x(p)).wait_recv()
 
+    def gf_copy(c):
+        q = second(c)
+        p = first(c)
+        return send(whole.at[q, c], whole.at[q, c], gx_s.at[x2, c], gx_r.at[q, c], dp=at_x(p))
+
+    def gx_both(c):
+        gx_copy(second(c), c).start()
+        gx_copy(first(c), c).start()
+
     each(1, NY, lambda k: gy_copy(yp(k)).start())
-    each(1, NX, lambda k: gx_copy(xp(k), y).start())
+    gx_both(y)
 
     def dy_copy(p):
         return send(dy_in.at[y], dy_in.at[y], dy_s.at[p], dy_r.at[y], dp=at_y(p))
@@ -271,7 +323,7 @@
     def pass_on(j):
         c = yp(j)
         gy_wait(c)
-        each(1, NX, lambda k: gx_copy(xp(k), c).start())
+        gx_both(c)
 
     each(1, NY // 2, pass_on)
 
@@ -290,46 +342,69 @@
     each(NY // 2, NY, pass_on)
 
     def dgz_copy(p):
-        return send(d_row, d_all.at[me], dgz_s.at[p], dgz_r.at[me], table=p)
+        return send(d_all.at[me], d_all.at[me], dgz_s.at[p], dgz_r.at[me], table=p)
 
     def dgz_wait(p):
-        send(d_row, d_all.at[p], dgz_s.at[p], dgz_r.at[p], table=p).wait_recv()
+        send(d_all.at[p], d_all.at[p], dgz_s.at[p], dgz_r.at[p], table=p).wait_recv()
+
+    def side_copy(p):
+        return send(d_all.at[p], d_all.at[p], side_s.at[p], dgz_r.at[p], table=side)
 
     each(1, NX, lambda k: dgx_wait(xp(k)))
-    each(1, nz, lambda k: dgz_copy(zp(k)).start())
     d_all[me] = d_row[...]
-
-    def gx_wait_all(k):
-        each(0, NY, lambda c: gx_wait(xp(k), c))
-
-    each(1, NX, gx_wait_all)
+    each(1, nz // 2, lambda k: dgz_copy(core(k)).start())
+    side_copy(me).start()
+
+    def forward(j):
+        c = yp(j)
+        gx_wait(second(c), c)
+        gf_copy(c).start()
+
+    each(0, NY, forward)
+
+    def gather_side(k):
+        p = core(k)
+        dgz_wait(p)
+        side_copy(p).start()
+
+    each(1, nz // 2, gather_side)
+
+    def gx_rest(c):
+        gx_wait(first(c), c)
+        gx_wait(x2, c)
+
+    each(0, NY, gx_rest)
     for px in range(NX):
         for c in range(NY):
             table_out[
                 px * x_rows + (c % 2) * half : px * x_rows + (c % 2 + 1) * half,
                 (c // 2) * 128 : (c // 2 + 1) * 128,
             ] = whole[px, c]
-    each(1, nz, lambda k: dgz_wait(zp(k)))
+    each(0, nz // 2, lambda k: dgz_wait(lax.rem(side + 2 * k, nz)))
     for t in range(nz):
         for c in range(NX):
             dense_out[t * cap : (t + 1) * cap, c * 128 : (c + 1) * 128] = d_all[t, c]
 
-    def sent_z(k):
-        p = zp(k)
-        z_copy(p).wait_send()
-        dz_copy(p).wait_send()
-        dgz_copy(p).wait_send()
+    def sent_side(k):
+        ds_copy(k).wait_send()
+        side_copy(core(k)).wait_send()
+
+    def sent_core(k):
+        dz_copy(k).wait_send()
+        dgz_copy(core(k)).wait_send()
 
     def sent_x(k):
         p = xp(k)
         dx_copy(p).wait_send()
         dgx_copy(p).wait_send()
 
-        def pieces(c):
-            x_copy(p, c).wait_send()
-            gx_copy(p, c).wait_send()
-
-        each(0, NY, pieces)
+    def sent_piece(c):
+        xa_copy(c).wait_send()
+        xb_copy(c).wait_send()
+        xc_copy(c).wait_send()
+        gx_copy(first(c), c).wait_send()
+        gx_copy(second(c), c).wait_send()
+        gf_copy(c).wait_send()
 
     def sent_y(k):
         p = yp(k)
@@ -337,7 +412,10 @@
         gy_copy(p).wait_send()
         dy_copy(p).wait_send()
 
-    each(1, nz, sent_z)
+    each(1, nz, lambda k: z_copy(zp(k)).wait_send())
+    each(0, nz // 2, sent_side)
+    each(1, nz // 2, sent_core)
+    each(0, NY, sent_piece)
     each(1, NX, sent_x)
     each(1, NY, sent_y)
 
@@ -363,7 +441,7 @@
         out_specs=(vmem, vmem),
         scratch_shapes=[
             pltpu.VMEM((groups, capacity, width), bf16),
-            pltpu.VMEM((groups, capacity, width), bf16),
+            pltpu.VMEM((groups // 2, capacity, width), bf16),
             pltpu.VMEM((NX, NY) + piece, bf16),
             pltpu.VMEM((NX, NY) + piece, bf16),
             pltpu.VMEM((NY,) + piece, bf16),
@@ -384,7 +462,14 @@
         + pair(NX)
         + pair(NY)
         + pair(NX)
-        + pair(groups),
+        + pair(groups)
+        + pair(groups // 2)
+        + [
+            dma((groups,)),
+            pltpu.VMEM((NY,) + piece, bf16),
+            pltpu.VMEM((groups // 2, capacity, width), bf16),
+            pltpu.VMEM((groups // 2, capacity, width), bf16),
+        ],
         compiler_params=pltpu.CompilerParams(
             collective_id=0, has_side_effects=True, vmem_limit_bytes=32 << 20
         ),

time: 128 us -> 125 us (0.977)
  Pallas kernels: 96.5 us -> 93.4 us
    pallas_call x1, Pallas kernels: 65.7 us -> 62.6 us  [exchange(): pl.pallas_call(functools.partial(exchange_kernel, scale), out_shape=(jax....]
where the time goes in v4:
time: 125 us
  Pallas kernels  93.4 us (75%)
  matrix products  17.3 us (14%)
  local copies, waits for them, and re-layouts  9.21 us (7%)
  other arithmetic  3.29 us (3%)
  between operations  1.67 us (1%)
    pallas_call x1, Pallas kernels, exchange(): pl.pallas_call(functools.partial(exchange_kernel, scale), out_shape=(jax....  62.6 us
    pallas_call x1, Pallas kernels, fetch(): pl.pallas_call(fetch_kernel, out_shape=(jax.ShapeDtypeStruct((slots, widt...  30.8 us
    dot_general x2, matrix products, hstu_layer(): jnp.dot(normed.reshape(samples_here * seq_span, model_width), w_in, prefe...  5.64 us
    dot_general x3, matrix products, hstu_layer(): jnp.einsum('blhd,bmhd->bhlm', queries.astype(jnp.float32), keys.astype(jn...  5.44 us
    unnamed x28, local copies, waits for them, and re-layouts  3.88 us
    dot_general x3, matrix products, hstu_layer(): jnp.einsum('bhlm,bmhd->blhd', weights.astype(jnp.float32), values.astype(...  3.4 us

profile of v4, /device:TPU:1, one launch (start us, length us, event | category | flops | bytes accessed | tf_op | source)
XLA Modules:
  0.0 125.0 jit_solution(7165042543607582517)
XLA Ops:
  0.6 0.0 copy-start
  1.5 0.0 copy-start.1
  1.5 1.1 copy-done.1
  2.6 0.7 copy-done.2
  3.3 0.7 copy-done.3
  4.0 30.8 %shard_map.86 = (bf16[256,512]{1,0:T(8,128)(2,1)S(1)}, s32[1,256]{1,0:T(1,128)S(1)}, s32[1,512]{1,0:T(1,128)S(1)}) custom-call(bf16[768,512]{1,0:T(8,128)(2,1)S(1)} %copy-done.1, s32[1,256]{1,0:T(1,128)S(1)} %bitcast.74, s32[1,256]{1,0:T(1,128)S(1)} %copy-done.3), custom_call_target="tpu_custom_call" | custom-call | tf_op jit(solution)/shard_map/pallas_call | solution.py:585
  34.8 0.1 convert_reduce_fusion
  35.0 0.2 fusion.35
  35.2 0.0 copy-done
  35.2 2.7 %fusion.66 = (bf16[256,2048]{1,0:T(8,128)(2,1)S(1)}, f32[256,2048]{1,0:T(8,128)}, f32[256,2048]{1,0:T(8,128)}) fusion(bf16[512,2048]{1,0:T(8,128)(2,1)S(1)} %copy-done, bf16[256,512]{1,0:T(8,128)(2,1)S(1)} %get-tuple-element.8, f32[256]{0:T(256)S(1)} %fusion.59, f32[256]{0:T(256)S(1)} %broadcast_multiply_fusion.1), kind=kOutput, calls=%fused_computation.96 | convolution fusion | flops 540016640 | bytes 7604224 | tf_op jit(solution)/shard_map/jvp()/dot_general | solution.py:29
  37.9 0.1 slice_bitcast_fusion
  38.0 0.0 copy-start.12
  38.0 0.1 copy.28
  38.1 0.0 copy-start.9
  38.1 0.1 copy.27
  38.3 0.0 copy-start.10
  38.3 1.6 %divide_convert_fusion = (bf16[4,256,256]{2,1,0:T(8,128)(2,1)S(1)}, f32[4,256,256]{2,1,0:T(8,128)}) fusion(f32[]{:T(128)} %bitcast.4, pred[256,256]{1,0:T(8,128)(4,1)S(1)} %fusion.56, bf16[256,4,128]{0,2,1:T(8,128)(2,1)S(1)} %bitcast.79, bf16[256,4,128]{0,2,1:T(8,128)(2,1)S(1)} %bitcast.77), kind=kOutput, calls=%fused_computation.36 | convolution fusion | flops 69206016 | bytes 2162692 | tf_op jit(solution)/shard_map/jvp(blhd,bmhd->bhlm)/dot_general | solution.py:40
  39.9 0.0 copy-done.9
  39.9 0.0 copy-done.10
  39.9 0.0 copy-done.12
  39.9 0.3 fusion.68
  40.2 0.4 copy-done.4
  40.7 0.1 fusion.39
  40.8 0.2 copy.22
  41.0 0.0 copy-start.6
  41.0 0.0 copy-start.7
  41.0 1.9 %multiply_reduce_fusion = (f32[256]{0:T(256)S(1)}, f32[256,512]{1,0:T(8,128)S(1)}) fusion(f32[256,512]{1,0:T(8,128)S(1)} %copy.22, f32[256]{0:T(256)S(1)} %broadcast_multiply_fusion, f32[256,2048]{1,0:T(8,128)} %get-tuple-element.15, bf16[512,512]{1,0:T(8,128)(2,1)} %param.12, bf16[1,256,512]{2,1,0:T(8,128)(2,1)} %param.13, ...), kind=kOutput, calls=%fused_computation.55 | convolution fusion | flops 135134976 | bytes 2361600 | tf_op jit(solution)/shard_map/transpose(jvp())/dot_general | solution.py:56
  42.9 0.1 copy-done.6
  43.0 0.5 convolution_convert_fusion.1
  43.4 1.0 fusion.65
  44.5 0.1 broadcast_add_fusion
  44.6 0.9 copy.23
  45.4 2.1 %fusion.26 = bf16[4,256,256]{2,1,0:T(8,128)(2,1)S(1)} fusion(f32[4,256,256]{2,1,0:T(8,128)} %get-tuple-element.24, bf16[4,128,256]{2,1,0:T(8,128)(2,1)} %bitcast.81, f32[]{:T(128)} %bitcast.4, pred[256,256]{1,0:T(8,128)(4,1)S(1)} %fusion.56, bf16[32,4,8,128]{3,2,1,0:T(8,128)(2,1)} %copy-done.12), kind=kOutput, calls=%fused_computation.32 | convolution fusion | flops 70778880 | bytes 2162692 | tf_op jit(solution)/shard_map/transpose(jvp(bhlm,bmhd->blhd))/dot_general | solution.py:52
  47.6 0.0 copy-done.5
  47.6 0.0 copy-done.11
  47.6 0.9 fusion.71
  48.5 1.8 %copy.26 = bf16[256,512]{1,0:T(8,128)(2,1)} copy(bf16[256,512]{0,1:T(8,128)(2,1)} %bitcast.84) | data formatting | bytes 524288 | tf_op jit(solution)/shard_map/transpose(jvp())/convert_element_type | solution.py:37
  50.3 2.0 %fusion.69 = bf16[4,256,128]{1,2,0:T(8,128)(2,1)} fusion(bf16[4,256,256]{2,1,0:T(8,128)(2,1)S(1)} %fusion.26, bf16[256,4,128]{0,2,1:T(8,128)(2,1)} %bitcast.78), kind=kOutput, calls=%fused_computation.98 | convolution fusion | flops 67108864 | bytes 1048576 | tf_op jit(solution)/shard_map/transpose(jvp(blhd,bmhd->bhlm))/dot_general | solution.py:40
  52.3 1.9 %fusion.70 = bf16[4,256,128]{1,2,0:T(8,128)(2,1)} fusion(bf16[4,256,256]{2,1,0:T(8,128)(2,1)S(1)} %fusion.26, bf16[256,4,128]{0,2,1:T(8,128)(2,1)} %bitcast.80), kind=kOutput, calls=%fused_computation.99 | convolution fusion | flops 67108864 | bytes 1048576 | tf_op jit(solution)/shard_map/transpose(jvp(blhd,bmhd->bhlm))/dot_general | solution.py:40
  54.2 1.1 copy.24
  55.3 1.1 copy.25
  56.4 0.0 copy-start.8
  56.4 2.9 %fusion.37 = (f32[256]{0:T(256)S(1)}, f32[256,512]{1,0:T(8,128)S(1)}) fusion(bf16[256,512]{1,0:T(8,128)(2,1)S(1)} %get-tuple-element.8, f32[256]{0:T(256)S(1)} %broadcast_multiply_fusion.1, bf16[512,2048]{1,0:T(8,128)(2,1)S(1)} %copy-done, f32[256,2048]{1,0:T(8,128)} %get-tuple-element.22, f32[256,512]{1,0:T(8,128)} %get-tuple-element.16, ...), kind=kOutput, calls=%fused_computation.49 | convolution fusion | flops 545521408 | bytes 6293504 | tf_op jit(solution)/shard_map/transpose(jvp())/dot_general | solution.py:29
  59.3 0.3 fusion.64
  59.6 0.5 convolution_convert_fusion.2
  60.2 62.6 %shard_map.87 = (bf16[768,512]{1,0:T(8,128)(2,1)S(1)}, bf16[512,512]{1,0:T(8,128)(2,1)S(1)}) custom-call(bf16[16,32,512]{2,1,0:T(8,128)(2,1)S(1)} %bitcast.73, bf16[16,32,512]{2,1,0:T(8,128)(2,1)S(1)} %bitcast.72, s32[1,512]{1,0:T(1,128)S(1)} %get-tuple-element.9.incoming), custom_call_target="tpu_custom_call" | custom-call | tf_op jit(solution)/shard_map/pallas_call | solution.py:434
  122.8 1.4 %convert_element_type.133 = f32[768,512]{1,0:T(8,128)} convert(bf16[768,512]{1,0:T(8,128)(2,1)S(1)} %get-tuple-element.10) | non-fusion elementwise | flops 393216 | bytes 2359296 | tf_op jit(solution)/shard_map/convert_element_type | solution.py:650
  124.2 0.8 copy.42
  (16 shorter events, 0.1 us)
Async XLA Ops:
  0.6 34.5 %copy-start = (bf16[512,2048]{1,0:T(8,128)(2,1)S(1)}, bf16[512,2048]{1,0:T(8,128)(2,1)}, u32[]{:S(2)}) copy-start(bf16[512,2048]{1,0:T(8,128)(2,1)} %param.11) | copy-start | bytes 6291460
  1.5 1.1 copy-start.1
  2.6 0.7 copy-start.2
  3.3 0.7 copy-start.3
  38.0 1.9 %copy-start.12 = (bf16[32,4,8,128]{3,2,1,0:T(8,128)(2,1)}, bf16[32,4,8,128]{3,2,1,0:T(8,128)(2,1)S(1)}, u32[]{:S(2)}) copy-start(bf16[32,4,8,128]{3,2,1,0:T(8,128)(2,1)S(1)} %get-tuple-element.17) | copy-start | bytes 786436
  38.1 1.7 %copy-start.9 = (bf16[256,512]{0,1:T(8,128)(2,1)}, bf16[256,512]{0,1:T(8,128)(2,1)S(1)}, u32[]{:S(2)}) copy-start(bf16[256,512]{0,1:T(8,128)(2,1)S(1)} %copy.28) | copy-start | bytes 786436
  38.3 1.6 %copy-start.10 = (bf16[256,512]{0,1:T(8,128)(2,1)}, bf16[256,512]{0,1:T(8,128)(2,1)S(1)}, u32[]{:S(2)}) copy-start(bf16[256,512]{0,1:T(8,128)(2,1)S(1)} %copy.27) | copy-start | bytes 786436
  39.9 0.8 copy-start.4
  41.0 2.0 %copy-start.6 = (f32[256,2048]{1,0:T(8,128)S(1)}, f32[256,2048]{1,0:T(8,128)}, u32[]{:S(2)}) copy-start(f32[256,2048]{1,0:T(8,128)} %get-tuple-element.15) | copy-start | bytes 6291460
  41.0 2.0 %copy-start.7 = (bf16[1,256,512]{2,1,0:T(8,128)(2,1)S(1)}, bf16[1,256,512]{2,1,0:T(8,128)(2,1)}, u32[]{:S(2)}) copy-start(bf16[1,256,512]{2,1,0:T(8,128)(2,1)} %param.13) | copy-start | bytes 786436
  45.4 2.1 %copy-start.5 = (bf16[4,256,256]{2,1,0:T(8,128)(2,1)S(1)}, bf16[4,256,256]{2,1,0:T(8,128)(2,1)}, u32[]{:S(2)}) copy-start(bf16[4,256,256]{2,1,0:T(8,128)(2,1)} %copy-done.4) | copy-start | bytes 1572868
  45.4 2.1 %copy-start.11 = (bf16[256,512]{0,1:T(8,128)(2,1)S(1)}, bf16[256,512]{0,1:T(8,128)(2,1)}, u32[]{:S(2)}) copy-start(bf16[256,512]{0,1:T(8,128)(2,1)} %copy.23) | copy-start | bytes 786436
  56.4 3.2 %copy-start.8 = (bf16[1,256,512]{2,1,0:T(8,128)(2,1)S(1)}, bf16[1,256,512]{2,1,0:T(8,128)(2,1)}, u32[]{:S(2)}) copy-start(bf16[1,256,512]{2,1,0:T(8,128)(2,1)} %param.13) | copy-start | bytes 786436

commit v5 on v4

--- a/solution.py
+++ b/solution.py
@@ -12,51 +12,6 @@
 NX = 4
 NY = 8
 MESH = pl.DeviceIdType.MESH
-
-
-def layer_norm(values):
-    average = jnp.mean(values, axis=-1, keepdims=True)
-    centred = values - average
-    variance = jnp.mean(centred * centred, axis=-1, keepdims=True)
-    return centred * lax.rsqrt(variance + 1e-06)
-
-
-def hstu_layer(embedded, w_in, w_out, lengths):
-    samples_here, seq_span, model_width = embedded.shape
-    head_dim = model_width // HEADS
-    normed = layer_norm(embedded.astype(jnp.float32)).astype(jnp.bfloat16)
-    projected = jax.nn.silu(
-        jnp.dot(
-            normed.reshape(samples_here * seq_span, model_width),
-            w_in,
-            preferred_element_type=jnp.float32,
-        )
-    )
-    gate_part = projected[:, :model_width]
-    shaped = (samples_here, seq_span, HEADS, head_dim)
-    values = projected[:, model_width : 2 * model_width].astype(jnp.bfloat16).reshape(shaped)
-    queries = projected[:, 2 * model_width : 3 * model_width].astype(jnp.bfloat16).reshape(shaped)
-    keys = projected[:, 3 * model_width :].astype(jnp.bfloat16).reshape(shaped)
-    scores = jnp.einsum(
-        "blhd,bmhd->bhlm", queries.astype(jnp.float32), keys.astype(jnp.float32)
-    ) * head_dim ** (-0.5)
-    positions = jnp.arange(seq_span)
-    live_keys = (positions[None, None, :] <= positions[None, :, None]) & (
-        positions[None, None, :] < lengths[:, None, None]
-    )
-    weights = (
-        jnp.where(live_keys[:, None], jax.nn.silu(scores), 0.0)
-        / lengths.astype(jnp.float32)[:, None, None, None]
-    )
-    weights = weights.astype(jnp.bfloat16)
-    attended = jnp.einsum(
-        "bhlm,bmhd->blhd", weights.astype(jnp.float32), values.astype(jnp.float32)
-    ).reshape(samples_here * seq_span, model_width)
-    mixed = (layer_norm(attended) * gate_part).astype(jnp.bfloat16)
-    output = jnp.dot(mixed, w_out, preferred_element_type=jnp.float32) + embedded.reshape(
-        -1, model_width
-    ).astype(jnp.float32)
-    return (output, mixed)
 
 
 def send(src, dst, send_sem, recv_sem, **where):
@@ -607,6 +562,114 @@
     )(table, owners, rows)
 
 
+def centre(values):
+    shifted = values - jnp.mean(values, axis=-1, keepdims=True)
+    spread = lax.rsqrt(jnp.mean(shifted * shifted, axis=-1, keepdims=True) + 1e-06)
+    return shifted * spread, spread
+
+
+def centre_back(grad, unit, spread):
+    along = jnp.mean(grad * unit, axis=-1, keepdims=True)
+    return spread * (grad - jnp.mean(grad, axis=-1, keepdims=True) - unit * along)
+
+
+def dot_last(a, b):
+    return lax.dot_general(a, b, (((1,), (1,)), ((), ())), preferred_element_type=jnp.float32)
+
+
+def dot_plain(a, b):
+    return jnp.dot(a, b, preferred_element_type=jnp.float32)
+
+
+def layer_kernel(
+    lengths, embedded, position, w_in, w_out, cotangent, outgoing, dense_part, before, after, grad
+):
+    f32, bf16 = jnp.float32, jnp.bfloat16
+    span, width = embedded.shape
+    head = width // HEADS
+    length = lengths[0]
+    share = 1.0 / length.astype(f32)
+    unit, spread = centre(embedded[...].astype(f32))
+    normed = unit.astype(bf16)
+    for b in range(4):
+        cols = slice(b * width, (b + 1) * width)
+        made = dot_plain(normed, w_in[:, cols])
+        before[:, cols] = made
+        if b > 0:
+            after[:, cols] = (made * jax.nn.sigmoid(made)).astype(bf16)
+    row = lax.broadcasted_iota(jnp.int32, (span, span), 0)
+    col = lax.broadcasted_iota(jnp.int32, (span, span), 1)
+    live = (col <= row) & (col < length)
+    scale = head ** (-0.5)
+
+    def columns(part, h):
+        return slice(part * width + h * head, part * width + (h + 1) * head)
+
+    attended = []
+    kept = []
+    for h in range(HEADS):
+        scores = dot_last(after[:, columns(2, h)], after[:, columns(3, h)]) * scale
+        gain = jax.nn.sigmoid(scores)
+        weights = (jnp.where(live, scores * gain, 0.0) * share).astype(bf16)
+        slope = jnp.where(live, gain * (1.0 + scores * (1.0 - gain)), 0.0) * share
+        attended.append(dot_plain(weights, after[:, columns(1, h)]))
+        kept.append((weights, slope))
+    mid, mid_spread = centre(jnp.concatenate(attended, axis=1))
+    gate_in = before[:, :width]
+    gate_sig = jax.nn.sigmoid(gate_in)
+    gate = gate_in * gate_sig
+    mixed = (mid * gate).astype(bf16)
+    item = lax.broadcasted_iota(jnp.int32, (span, width), 0)
+    seed = jnp.where(item < length, cotangent[...].astype(f32), 0.0)
+    seed_low = seed.astype(bf16)
+    dense_part[...] = dot_first(mixed, seed_low).astype(bf16)
+
+    d_mixed = dot_last(seed_low, w_out[...]).astype(bf16).astype(f32)
+    grad[:, :width] = (d_mixed * mid * (gate_sig * (1.0 + gate_in * (1.0 - gate_sig)))).astype(bf16)
+    d_att = centre_back(d_mixed * gate, mid, mid_spread).astype(bf16)
+
+    def keep(part, h, value):
+        cols = columns(part, h)
+        x = before[:, cols]
+        sig = jax.nn.sigmoid(x)
+        grad[:, cols] = (value * (sig * (1.0 + x * (1.0 - sig)))).astype(bf16)
+
+    for h in range(HEADS):
+        weights, slope = kept[h]
+        d_head = d_att[:, h * head : (h + 1) * head]
+        d_scores = (dot_last(d_head, after[:, columns(1, h)]) * slope * scale).astype(bf16)
+        keep(1, h, dot_first(weights, d_head))
+        keep(2, h, dot_plain(d_scores, after[:, columns(3, h)]))
+        keep(3, h, dot_first(d_scores, after[:, columns(2, h)]))
+    d_normed = dot_last(grad[:, :width], w_in[:, :width])
+    for b in range(1, 4):
+        cols = slice(b * width, (b + 1) * width)
+        d_normed = d_normed + dot_last(grad[:, cols], w_in[:, cols])
+    row_grad = (centre_back(d_normed, unit, spread) + seed).astype(bf16)
+    spots = hot((outgoing.shape[0], span), position[...])
+    outgoing[...] = dot_plain(spots, row_grad).astype(bf16)
+
+
+def layer(lengths, embedded, position, w_in, w_out, cotangent, spots):
+    span, width = embedded.shape
+    vmem = pl.BlockSpec(memory_space=pltpu.VMEM)
+    return pl.pallas_call(
+        layer_kernel,
+        out_shape=(
+            jax.ShapeDtypeStruct((spots, width), jnp.bfloat16),
+            jax.ShapeDtypeStruct((width, width), jnp.bfloat16),
+        ),
+        in_specs=[pl.BlockSpec(memory_space=pltpu.SMEM)] + [vmem] * 5,
+        out_specs=(vmem, vmem),
+        scratch_shapes=[
+            pltpu.VMEM((span, 4 * width), jnp.float32),
+            pltpu.VMEM((span, 4 * width), jnp.bfloat16),
+            pltpu.VMEM((span, 4 * width), jnp.bfloat16),
+        ],
+        compiler_params=pltpu.CompilerParams(vmem_limit_bytes=40 << 20),
+    )(lengths, embedded, position, w_in, w_out, cotangent)
+
+
 def per_device(table, history_shard, history_row, lengths, w_in, w_out, cotangent):
     shard_rows, model_width = table.shape
     samples_here, seq_span = history_row.shape
@@ -621,25 +684,17 @@
         groups,
         capacity,
     )
-    slots_at = jnp.arange(groups * capacity, dtype=jnp.int32)[:, None]
-    place = (slots_at == position).astype(jnp.bfloat16)
-    embedded = embedded.reshape(samples_here, seq_span, model_width)
-    output, pullback, mixed = jax.vjp(
-        lambda rows_in: hstu_layer(rows_in, w_in, w_out, lengths), embedded, has_aux=True
+    outgoing, dense_part = layer(
+        lengths,
+        embedded,
+        position,
+        w_in,
+        w_out,
+        cotangent.reshape(slot_count, model_width),
+        groups * capacity,
     )
-    row_live = jnp.arange(seq_span)[None, :] < lengths[:, None]
-    grad_seed = jnp.where(row_live[:, :, None], cotangent, jnp.zeros_like(cotangent))
-    flat_seed = grad_seed.reshape(-1, model_width)
-
     total_slots = slot_count * copies * groups
     grad_scale = 1.0 / math.sqrt(total_slots)
-    dense_part = lax.dot_general(
-        mixed, flat_seed, (((0,), (0,)), ((), ())), preferred_element_type=jnp.float32
-    ).astype(jnp.bfloat16)
-    (row_grad,) = pullback(flat_seed.astype(jnp.float32))
-    outgoing = jnp.dot(
-        place, row_grad.reshape(-1, model_width), preferred_element_type=jnp.float32
-    ).astype(jnp.bfloat16)
     table_sum, dense_grad = exchange(
         outgoing.reshape(groups, capacity, model_width),
         dense_part.reshape(groups, capacity, model_width),

time: 125 us -> 108 us (0.86)
  matrix products: 17.3 us -> 0 us
  Pallas kernels: 93.4 us -> 97.7 us
  local copies, waits for them, and re-layouts: 9.21 us -> 6.85 us
  other arithmetic: 3.29 us -> 1.35 us
    dot_general x11 -> x0, matrix products: 17.3 us -> none  [the longest x2 5.64 us: hstu_layer(): jnp.dot(normed.reshape(samples_here * seq_span, model_width), w_in, prefe...]
    pallas_call x0 -> x1, Pallas kernels: none -> 4.47 us  [layer(): pl.pallas_call(layer_kernel, out_shape=(jax.ShapeDtypeStruct((spots, widt...]
    convert_element_type x3 -> x0, local copies, waits for them, and re-layouts: 4 us -> none  [the longest x1 1.82 us: hstu_layer(): projected[:, model_width:2 * model_width].astype(jnp.bfloat16)]
    unnamed x28 -> x13, local copies, waits for them, and re-layouts: 3.88 us -> 6.85 us
    reduce_sum x5 -> x0, other arithmetic: 1.73 us -> none  [the longest x2 1.3 us: layer_norm(): centred = values - average]
where the time goes in v5:
time: 108 us; the launch traced here: 107 us
  Pallas kernels  97.7 us (90%)
  local copies, waits for them, and re-layouts  6.85 us (6%)
  other arithmetic  1.35 us (1%)
  between operations  1.32 us (1%)
    pallas_call x1, Pallas kernels, exchange(): pl.pallas_call(functools.partial(exchange_kernel, scale), out_shape=(jax....  62.4 us
    pallas_call x1, Pallas kernels, fetch(): pl.pallas_call(fetch_kernel, out_shape=(jax.ShapeDtypeStruct((slots, widt...  30.8 us
    unnamed x13, local copies, waits for them, and re-layouts  6.85 us
    pallas_call x1, Pallas kernels, layer(): pl.pallas_call(layer_kernel, out_shape=(jax.ShapeDtypeStruct((spots, widt...  4.47 us

profile of v5, /device:TPU:1, one launch (start us, length us, event | category | flops | bytes accessed | tf_op | source)
XLA Modules:
  0.0 107.2 jit_solution(15053234524808874515)
XLA Ops:
  1.3 0.0 copy-start.1
  1.3 1.1 %copy-done.1 = bf16[768,512]{1,0:T(8,128)(2,1)S(1)} copy-done((bf16[768,512]{1,0:T(8,128)(2,1)S(1)}, bf16[768,512]{1,0:T(8,128)(2,1)}, u32[]{:S(2)}) %copy-start.1) | copy-done | bytes 786456
  2.4 0.0 copy-start.4
  2.4 0.7 copy-done.4
  3.1 0.0 copy-start.5
  3.1 0.7 copy-done.5
  3.8 30.8 %shard_map.86 = (bf16[256,512]{1,0:T(8,128)(2,1)S(1)}, s32[1,256]{1,0:T(1,128)S(1)}, s32[1,512]{1,0:T(1,128)S(1)}) custom-call(bf16[768,512]{1,0:T(8,128)(2,1)S(1)} %copy-done.1, s32[1,256]{1,0:T(1,128)S(1)} %bitcast.7, s32[1,256]{1,0:T(1,128)S(1)} %copy-done.5), custom_call_target="tpu_custom_call" | custom-call | tf_op jit(solution)/shard_map/pallas_call | solution.py:540
  34.6 0.0 copy-start
  34.6 1.6 %copy-done = bf16[512,2048]{1,0:T(8,128)(2,1)S(1)} copy-done((bf16[512,2048]{1,0:T(8,128)(2,1)S(1)}, bf16[512,2048]{1,0:T(8,128)(2,1)}, u32[]{:S(2)}) %copy-start) | copy-done | bytes 2097176
  36.2 0.0 copy-start.2
  36.2 1.0 copy-done.2
  37.2 0.0 copy-start.3
  37.3 0.9 copy-done.3
  38.2 4.5 %shard_map.87 = (bf16[512,512]{1,0:T(8,128)(2,1)S(1)}, bf16[512,512]{1,0:T(8,128)(2,1)S(1)}) custom-call(s32[1]{0:T(128)S(6)} %copy.10.lengths, bf16[256,512]{1,0:T(8,128)(2,1)S(1)} %get-tuple-element.9.embedded, s32[1,256]{1,0:T(1,128)S(1)} %get-tuple-element.10.position, bf16[512,2048]{1,0:T(8,128)(2,1)S(1)} %copy-done, bf16[512,512]{1,0:T(8,128)(2,1)S(1)} %copy-done.2, ...), custom_call_target="tpu_custom_call" | custom-call | tf_op jit(solution)/shard_map/pallas_call | solution.py:656
  42.7 62.4 %shard_map.88 = (bf16[768,512]{1,0:T(8,128)(2,1)S(1)}, bf16[512,512]{1,0:T(8,128)(2,1)S(1)}) custom-call(bf16[16,32,512]{2,1,0:T(8,128)(2,1)S(1)} %bitcast.4, bf16[16,32,512]{2,1,0:T(8,128)(2,1)S(1)} %bitcast.5, s32[1,512]{1,0:T(1,128)S(1)} %get-tuple-element.13.incoming), custom_call_target="tpu_custom_call" | custom-call | tf_op jit(solution)/shard_map/pallas_call | solution.py:389
  105.0 1.4 %convert_element_type.3 = f32[768,512]{1,0:T(8,128)} convert(bf16[768,512]{1,0:T(8,128)(2,1)S(1)} %get-tuple-element.14) | non-fusion elementwise | flops 393216 | bytes 2359296 | tf_op jit(solution)/shard_map/convert_element_type | solution.py:705
  106.4 0.8 copy.11
Async XLA Ops:
  1.3 1.1 %copy-start.1 = (bf16[768,512]{1,0:T(8,128)(2,1)S(1)}, bf16[768,512]{1,0:T(8,128)(2,1)}, u32[]{:S(2)}) copy-start(bf16[768,512]{1,0:T(8,128)(2,1)} %table.1) | copy-start | bytes 2359300
  2.4 0.7 copy-start.4
  3.1 0.7 copy-start.5
  34.6 1.6 %copy-start = (bf16[512,2048]{1,0:T(8,128)(2,1)S(1)}, bf16[512,2048]{1,0:T(8,128)(2,1)}, u32[]{:S(2)}) copy-start(bf16[512,2048]{1,0:T(8,128)(2,1)} %w_in.1) | copy-start | bytes 6291460
  36.2 1.0 copy-start.2
  37.2 0.9 copy-start.3

commit v6 on v5

--- a/solution.py
+++ b/solution.py
@@ -118,16 +118,6 @@
     def at_y(py):
         return x * NY + py
 
-    barrier = pltpu.get_barrier_semaphore()
-
-    def greet(axis, peer):
-        pl.semaphore_signal(barrier, inc=1, device_id={axis: peer}, device_id_type=MESH)
-
-    each(1, nz, lambda k: greet("table", zp(k)))
-    each(1, NX, lambda k: greet("dp", at_x(xp(k))))
-    each(1, NY, lambda k: greet("dp", at_y(yp(k))))
-    pl.semaphore_wait(barrier, nz - 1 + NX - 1 + NY - 1)
-
     def z_copy(p):
         return send(outgoing.at[p], arrived.at[me], z_s.at[p], z_r.at[me], table=p)
 
@@ -375,62 +365,6 @@
     each(1, NY, sent_y)
 
 
-def exchange(outgoing, dense_part, incoming, shard_rows, scale):
-    groups, capacity, width = outgoing.shape
-    bf16 = jnp.bfloat16
-    piece = (shard_rows // NX // 2, 128)
-    small = (capacity, 128)
-    vmem = pl.BlockSpec(memory_space=pltpu.VMEM)
-    dma = pltpu.SemaphoreType.DMA
-
-    def pair(*dims):
-        return [dma(dims), dma(dims)]
-
-    return pl.pallas_call(
-        functools.partial(exchange_kernel, scale),
-        out_shape=(
-            jax.ShapeDtypeStruct((shard_rows, width), bf16),
-            jax.ShapeDtypeStruct((groups * capacity, width), bf16),
-        ),
-        in_specs=[vmem] * 3,
-        out_specs=(vmem, vmem),
-        scratch_shapes=[
-            pltpu.VMEM((groups, capacity, width), bf16),
-            pltpu.VMEM((groups // 2, capacity, width), bf16),
-            pltpu.VMEM((NX, NY) + piece, bf16),
-            pltpu.VMEM((NX, NY) + piece, bf16),
-            pltpu.VMEM((NY,) + piece, bf16),
-            pltpu.VMEM((NY,) + piece, bf16),
-            pltpu.VMEM((NX, NY) + piece, bf16),
-            pltpu.VMEM((NX,) + small, bf16),
-            pltpu.VMEM((NX,) + small, bf16),
-            pltpu.VMEM((NY,) + small, bf16),
-            pltpu.VMEM((NX,) + small, bf16),
-            pltpu.VMEM((groups, NX) + small, bf16),
-        ]
-        + pair(groups)
-        + pair(groups)
-        + pair(NX, NY)
-        + pair(NY)
-        + pair(NY)
-        + pair(NX, NY)
-        + pair(NX)
-        + pair(NY)
-        + pair(NX)
-        + pair(groups)
-        + pair(groups // 2)
-        + [
-            dma((groups,)),
-            pltpu.VMEM((NY,) + piece, bf16),
-            pltpu.VMEM((groups // 2, capacity, width), bf16),
-            pltpu.VMEM((groups // 2, capacity, width), bf16),
-        ],
-        compiler_params=pltpu.CompilerParams(
-            collective_id=0, has_side_effects=True, vmem_limit_bytes=32 << 20
-        ),
-    )(outgoing, dense_part, incoming)
-
-
 def dot_first(a, b):
     return lax.dot_general(a, b, (((0,), (0,)), ((), ())), preferred_element_type=jnp.float32)
 
@@ -441,6 +375,8 @@
 
 
 def fetch_kernel(
+    ready,
+    table_here,
     table,
     owners,
     rows,
@@ -466,14 +402,6 @@
     def zp(k):
         return lax.rem(me + k, nz)
 
-    barrier = pltpu.get_barrier_semaphore()
-    each(
-        1,
-        nz,
-        lambda k: pl.semaphore_signal(
-            barrier, inc=1, device_id={"table": zp(k)}, device_id_type=MESH
-        ),
-    )
     own = owners[...]
     hits = (lax.broadcasted_iota(jnp.int32, (nz, slots), 0) == own).astype(f32)
     earlier = (
@@ -494,7 +422,7 @@
     asked = (found[0:1] * 256.0 + found[1:2]).astype(jnp.int32)
     for p in range(nz):
         req_out[p] = asked[:, p * 128 : (p + 1) * 128]
-    pl.semaphore_wait(barrier, nz - 1)
+    ready()
 
     def q_copy(p):
         return send(req_out.at[p], req_in.at[me], q_s.at[p], q_r.at[me], table=p)
@@ -511,6 +439,7 @@
     each(1, nz, lambda k: q_copy(zp(k)).start())
     req_in[me] = req_out[me]
     each(1, nz, lambda k: q_wait(zp(k)))
+    table_here()
     for g in range(nz // per):
         line = req_in[g * per]
         for j in range(1, per):
@@ -530,36 +459,6 @@
         r_copy(zp(k)).wait_send()
 
     each(1, nz, sent)
-
-
-def fetch(table, owners, rows, groups, capacity):
-    shard_rows, width = table.shape
-    slots = owners.shape[1]
-    vmem = pl.BlockSpec(memory_space=pltpu.VMEM)
-    dma = pltpu.SemaphoreType.DMA
-    return pl.pallas_call(
-        fetch_kernel,
-        out_shape=(
-            jax.ShapeDtypeStruct((slots, width), jnp.bfloat16),
-            jax.ShapeDtypeStruct((1, slots), jnp.int32),
-            jax.ShapeDtypeStruct((1, groups * capacity), jnp.int32),
-        ),
-        in_specs=[vmem] * 3,
-        out_specs=(vmem, vmem, vmem),
-        scratch_shapes=[
-            pltpu.VMEM((groups, 1, 128), jnp.int32),
-            pltpu.VMEM((groups, 1, 128), jnp.int32),
-            pltpu.VMEM((groups, capacity, width), jnp.bfloat16),
-            pltpu.VMEM((groups, capacity, width), jnp.bfloat16),
-            dma((groups,)),
-            dma((groups,)),
-            dma((groups,)),
-            dma((groups,)),
-        ],
-        compiler_params=pltpu.CompilerParams(
-            collective_id=1, has_side_effects=True, vmem_limit_bytes=32 << 20
-        ),
-    )(table, owners, rows)
 
 
 def centre(values):
@@ -622,7 +521,7 @@
     item = lax.broadcasted_iota(jnp.int32, (span, width), 0)
     seed = jnp.where(item < length, cotangent[...].astype(f32), 0.0)
     seed_low = seed.astype(bf16)
-    dense_part[...] = dot_first(mixed, seed_low).astype(bf16)
+    dense_part[...] = dot_first(mixed, seed_low).astype(bf16).reshape(dense_part.shape)
 
     d_mixed = dot_last(seed_low, w_out[...]).astype(bf16).astype(f32)
     grad[:, :width] = (d_mixed * mid * (gate_sig * (1.0 + gate_in * (1.0 - gate_sig)))).astype(bf16)
@@ -646,28 +545,156 @@
         cols = slice(b * width, (b + 1) * width)
         d_normed = d_normed + dot_last(grad[:, cols], w_in[:, cols])
     row_grad = (centre_back(d_normed, unit, spread) + seed).astype(bf16)
-    spots = hot((outgoing.shape[0], span), position[...])
-    outgoing[...] = dot_plain(spots, row_grad).astype(bf16)
-
-
-def layer(lengths, embedded, position, w_in, w_out, cotangent, spots):
-    span, width = embedded.shape
+    nz, cap, _ = outgoing.shape
+    spots = hot((nz * cap, span), position[...])
+    outgoing[...] = dot_plain(spots, row_grad).astype(bf16).reshape(outgoing.shape)
+
+
+def step_kernel(
+    scale,
+    lengths,
+    table_far,
+    owners,
+    rows,
+    w_in_far,
+    w_out_far,
+    cotangent_far,
+    table_out,
+    dense_out,
+    table,
+    w_in,
+    w_out,
+    cotangent,
+    near_s,
+    embedded,
+    position,
+    incoming,
+    outgoing,
+    dense_part,
+    *scratch,
+):
+    nz = outgoing.shape[0]
+    me = lax.axis_index("table")
+    spot = lax.axis_index("dp")
+    x = spot // NY
+    y = lax.rem(spot, NY)
+    barrier = pltpu.get_barrier_semaphore()
+
+    def greet(axis, peer):
+        pl.semaphore_signal(barrier, inc=1, device_id={axis: peer}, device_id_type=MESH)
+
+    each(1, nz, lambda k: greet("table", lax.rem(me + k, nz)))
+    each(1, NX, lambda k: greet("dp", lax.rem(x + k, NX) * NY + y))
+    each(1, NY, lambda k: greet("dp", x * NY + lax.rem(y + k, NY)))
+
+    pairs = ((table_far, table), (w_in_far, w_in), (w_out_far, w_out), (cotangent_far, cotangent))
+    copies = [pltpu.make_async_copy(a, b, near_s.at[i]) for i, (a, b) in enumerate(pairs)]
+    for copy in copies:
+        copy.start()
+
+    def ready():
+        pl.semaphore_wait(barrier, nz - 1 + NX - 1 + NY - 1)
+
+    fetch_kernel(
+        ready, copies[0].wait, table, owners, rows, embedded, position, incoming, *scratch[:8]
+    )
+    for copy in copies[1:]:
+        copy.wait()
+    layer_kernel(
+        lengths,
+        embedded,
+        position,
+        w_in,
+        w_out,
+        cotangent,
+        outgoing,
+        dense_part,
+        *scratch[8:11],
+    )
+    exchange_kernel(
+        scale, outgoing, dense_part, incoming, table_out, dense_out, *scratch[11:]
+    )
+
+
+def step(lengths, table, owners, rows, w_in, w_out, cotangent, groups, capacity, scale):
+    shard_rows, width = table.shape
+    slots = owners.shape[1]
+    bf16, f32, i32 = jnp.bfloat16, jnp.float32, jnp.int32
+    piece = (shard_rows // NX // 2, 128)
+    small = (capacity, 128)
+    block = (groups, capacity, width)
     vmem = pl.BlockSpec(memory_space=pltpu.VMEM)
+    far = pl.BlockSpec(memory_space=pl.ANY)
+    dma = pltpu.SemaphoreType.DMA
+    room = pltpu.VMEM
+
+    def pair(*dims):
+        return [dma(dims), dma(dims)]
+
     return pl.pallas_call(
-        layer_kernel,
+        functools.partial(step_kernel, scale),
         out_shape=(
-            jax.ShapeDtypeStruct((spots, width), jnp.bfloat16),
-            jax.ShapeDtypeStruct((width, width), jnp.bfloat16),
+            jax.ShapeDtypeStruct((shard_rows, width), bf16),
+            jax.ShapeDtypeStruct((groups * capacity, width), bf16),
         ),
-        in_specs=[pl.BlockSpec(memory_space=pltpu.SMEM)] + [vmem] * 5,
+        in_specs=[pl.BlockSpec(memory_space=pltpu.SMEM), far, vmem, vmem, far, far, far],
         out_specs=(vmem, vmem),
         scratch_shapes=[
-            pltpu.VMEM((span, 4 * width), jnp.float32),
-            pltpu.VMEM((span, 4 * width), jnp.bfloat16),
-            pltpu.VMEM((span, 4 * width), jnp.bfloat16),
+            room(table.shape, bf16),
+            room(w_in.shape, bf16),
+            room(w_out.shape, bf16),
+            room(cotangent.shape, bf16),
+            dma((4,)),
+            room((slots, width), bf16),
+            room((1, slots), i32),
+            room((1, groups * capacity), i32),
+            room(block, bf16),
+            room(block, bf16),
+            room((groups, 1, 128), i32),
+            room((groups, 1, 128), i32),
+            room(block, bf16),
+            room(block, bf16),
+        ]
+        + pair(groups)
+        + pair(groups)
+        + [
+            room((slots, 4 * width), f32),
+            room((slots, 4 * width), bf16),
+            room((slots, 4 * width), bf16),
+            room(block, bf16),
+            room((groups // 2, capacity, width), bf16),
+            room((NX, NY) + piece, bf16),
+            room((NX, NY) + piece, bf16),
+            room((NY,) + piece, bf16),
+            room((NY,) + piece, bf16),
+            room((NX, NY) + piece, bf16),
+            room((NX,) + small, bf16),
+            room((NX,) + small, bf16),
+            room((NY,) + small, bf16),
+            room((NX,) + small, bf16),
+            room((groups, NX) + small, bf16),
+        ]
+        + pair(groups)
+        + pair(groups)
+        + pair(NX, NY)
+        + pair(NY)
+        + pair(NY)
+        + pair(NX, NY)
+        + pair(NX)
+        + pair(NY)
+        + pair(NX)
+        + pair(groups)
+        + pair(groups // 2)
+        + [
+            dma((groups,)),
+            room((NY,) + piece, bf16),
+            room((groups // 2, capacity, width), bf16),
+            room((groups // 2, capacity, width), bf16),
         ],
-        compiler_params=pltpu.CompilerParams(vmem_limit_bytes=40 << 20),
-    )(lengths, embedded, position, w_in, w_out, cotangent)
+        compiler_params=pltpu.CompilerParams(
+            collective_id=0, has_side_effects=True, vmem_limit_bytes=60 << 20
+        ),
+    )(lengths, table, owners, rows, w_in, w_out, cotangent)
 
 
 def per_device(table, history_shard, history_row, lengths, w_in, w_out, cotangent):
@@ -677,29 +704,18 @@
     copies = lax.axis_size("dp")
     slot_count = samples_here * seq_span
     capacity = 2 * slot_count // groups
-    embedded, position, incoming = fetch(
+    total_slots = slot_count * copies * groups
+    grad_scale = 1.0 / math.sqrt(total_slots)
+    table_sum, dense_grad = step(
+        lengths,
         table,
         history_shard.reshape(1, slot_count),
         history_row.reshape(1, slot_count),
-        groups,
-        capacity,
-    )
-    outgoing, dense_part = layer(
-        lengths,
-        embedded,
-        position,
         w_in,
         w_out,
         cotangent.reshape(slot_count, model_width),
-        groups * capacity,
-    )
-    total_slots = slot_count * copies * groups
-    grad_scale = 1.0 / math.sqrt(total_slots)
-    table_sum, dense_grad = exchange(
-        outgoing.reshape(groups, capacity, model_width),
-        dense_part.reshape(groups, capacity, model_width),
-        incoming,
-        shard_rows,
+        groups,
+        capacity,
         grad_scale,
     )
     table_grad = table_sum.astype(jnp.float32)

time: 108 us -> 99.2 us (0.919)
  local copies, waits for them, and re-layouts: 6.85 us -> 0.8 us
  Pallas kernels: 97.7 us -> 94.4 us
  other arithmetic: 1.35 us -> 2.55 us
    unnamed x13 -> x3, local copies, waits for them, and re-layouts: 6.85 us -> 0.8 us
    pallas_call x3 -> x1, Pallas kernels: 97.7 us -> 94.4 us  [step(): pl.pallas_call(functools.partial(step_kernel, scale), out_shape=(jax.Shap...]
    convert_element_type x1, other arithmetic: 1.35 us -> 2.55 us  [per_device(): table_grad = table_sum.astype(jnp.float32)]
where the time goes in v6:
time: 99.2 us; the launch traced here: 99 us
  Pallas kernels  94.4 us (95%)
  other arithmetic  2.55 us (3%)
  between operations  1.29 us (1%)
    pallas_call x1, Pallas kernels, step(): pl.pallas_call(functools.partial(step_kernel, scale), out_shape=(jax.Shap...  94.4 us
    convert_element_type x1, other arithmetic, per_device(): table_grad = table_sum.astype(jnp.float32)  2.55 us

profile of v6, /device:TPU:1, one launch (start us, length us, event | category | flops | bytes accessed | tf_op | source)
XLA Modules:
  0.0 99.0 jit_solution(1194953378423996410)
XLA Ops:
  1.3 94.4 %shard_map.86 = (bf16[768,512]{1,0:T(8,128)(2,1)}, bf16[512,512]{1,0:T(8,128)(2,1)}) custom-call(s32[1]{0:T(128)S(6)} %copy.10.lengths, bf16[768,512]{1,0:T(8,128)(2,1)} %table_far.1, s32[1,256]{1,0:T(1,128)} %bitcast.3, s32[1,256]{1,0:T(1,128)} %rows.1, bf16[512,2048]{1,0:T(8,128)(2,1)} %w_in_far.1, bf16[512,512]{1,0:T(8,128)(2,1)} %w_out_far.1, ...), custom_call_target="tpu_custom_call" | custom-call | tf_op jit(solution)/shard_map/pallas_call | solution.py:634
  95.7 0.0 copy-start
  95.7 2.5 %convert_element_type.3 = f32[768,512]{1,0:T(8,128)} convert(bf16[768,512]{1,0:T(8,128)(2,1)} %get-tuple-element.4) | non-fusion elementwise | flops 393216 | bytes 2359296 | tf_op jit(solution)/shard_map/convert_element_type | solution.py:721
  98.2 0.0 copy-done
  98.2 0.8 copy.11
Async XLA Ops:
  95.7 2.6 %copy-start = (bf16[512,512]{1,0:T(8,128)(2,1)S(1)}, bf16[512,512]{1,0:T(8,128)(2,1)}, u32[]{:S(2)}) copy-start(bf16[512,512]{1,0:T(8,128)(2,1)} %get-tuple-element.9) | copy-start | bytes 1572868

commit v7 on v6

--- a/solution.py
+++ b/solution.py
@@ -78,6 +78,7 @@
     x_mid,
     d_side,
     d_pair,
+    d_mid,
 ):
     nz, cap, width = outgoing.shape
     rows = table_out.shape[0]
@@ -129,7 +130,7 @@
         return send(dense_part.at[p], d_side.at[k], ds_s.at[k], ds_r.at[k], table=side)
 
     def dz_copy(k):
-        return send(d_pair.at[k], dense_arr.at[k], dz_s.at[k], dz_r.at[k], table=core(k))
+        return send(d_mid.at[k], dense_arr.at[k], dz_s.at[k], dz_r.at[k], table=core(k))
 
     each(1, nz, lambda k: z_copy(zp(k)).start())
     each(0, nz // 2, lambda k: ds_copy(k).start())
@@ -140,7 +141,22 @@
         mine = dense_part[core(k)].astype(f32) + d_side[k].astype(f32)
         d_pair[k] = mine.astype(bf16)
 
+    def dx_copy(p):
+        return send(dx_out.at[p], dx_in.at[x], dx_s.at[p], dx_r.at[x], dp=at_x(p))
+
+    def dx_wait(p):
+        send(dx_out.at[p], dx_in.at[p], dx_s.at[p], dx_r.at[p], dp=at_x(p)).wait_recv()
+
     each(0, nz // 2, pair_up)
+    for c in range(NX):
+        dx_out[c] = d_pair[:, :, c * 128 : (c + 1) * 128]
+    each(1, NX, lambda k: dx_copy(xp(k)).start())
+    dx_in[x] = dx_out[x]
+    each(1, NX, lambda k: dx_wait(xp(k)))
+    d_total = dx_in[0].astype(f32)
+    for k in range(1, NX):
+        d_total = d_total + dx_in[k].astype(f32)
+    d_mid[...] = d_total.astype(bf16)
     each(1, nz, lambda k: z_wait(zp(k)))
     each(1, nz // 2, lambda k: dz_copy(k).start())
 
@@ -205,20 +221,18 @@
     each(1, NY, y_stage)
     sum_x(y)
 
-    def dx_copy(p):
-        return send(dx_out.at[p], dx_in.at[x], dx_s.at[p], dx_r.at[x], dp=at_x(p))
-
-    def dx_wait(p):
-        send(dx_out.at[p], dx_in.at[p], dx_s.at[p], dx_r.at[p], dp=at_x(p)).wait_recv()
+    def dy_copy(p):
+        return send(dy_in.at[y], dy_in.at[y], dy_s.at[p], dy_r.at[y], dp=at_y(p))
+
+    def dy_wait(p):
+        send(dy_in.at[p], dy_in.at[p], dy_s.at[p], dy_r.at[p], dp=at_y(p)).wait_recv()
 
     each(1, nz // 2, lambda k: dz_copy(k).wait_recv())
-    dense_sum = d_pair[0].astype(f32)
+    d_total = d_mid[0].astype(f32)
     for k in range(1, nz // 2):
-        dense_sum = dense_sum + dense_arr[k].astype(f32)
-    dense_sum = dense_sum.astype(bf16)
-    for c in range(NX):
-        dx_out[c] = dense_sum[:, c * 128 : (c + 1) * 128]
-    each(1, NX, lambda k: dx_copy(xp(k)).start())
+        d_total = d_total + dense_arr[k].astype(f32)
+    dy_in[y] = d_total.astype(bf16)
+    each(1, NY, lambda k: dy_copy(yp(k)).start())
 
     total = x_sum[y].astype(f32)
     for j in range(1, NY):
@@ -250,20 +264,6 @@
 
     each(1, NY, lambda k: gy_copy(yp(k)).start())
     gx_both(y)
-
-    def dy_copy(p):
-        return send(dy_in.at[y], dy_in.at[y], dy_s.at[p], dy_r.at[y], dp=at_y(p))
-
-    def dy_wait(p):
-        send(dy_in.at[p], dy_in.at[p], dy_s.at[p], dy_r.at[p], dp=at_y(p)).wait_recv()
-
-    dx_in[x] = dx_out[x]
-    each(1, NX, lambda k: dx_wait(xp(k)))
-    d_total = dx_in[0].astype(f32)
-    for k in range(1, NX):
-        d_total = d_total + dx_in[k].astype(f32)
-    dy_in[y] = d_total.astype(bf16)
-    each(1, NY, lambda k: dy_copy(yp(k)).start())
 
     def pass_on(j):
         c = yp(j)
@@ -662,14 +662,14 @@
             room((slots, 4 * width), bf16),
             room((slots, 4 * width), bf16),
             room(block, bf16),
-            room((groups // 2, capacity, width), bf16),
+            room((groups // 2,) + small, bf16),
             room((NX, NY) + piece, bf16),
             room((NX, NY) + piece, bf16),
             room((NY,) + piece, bf16),
             room((NY,) + piece, bf16),
             room((NX, NY) + piece, bf16),
-            room((NX,) + small, bf16),
-            room((NX,) + small, bf16),
+            room((NX, groups // 2) + small, bf16),
+            room((NX, groups // 2) + small, bf16),
             room((NY,) + small, bf16),
             room((NX,) + small, bf16),
             room((groups, NX) + small, bf16),
@@ -690,6 +690,7 @@
             room((NY,) + piece, bf16),
             room((groups // 2, capacity, width), bf16),
             room((groups // 2, capacity, width), bf16),
+            room((groups // 2,) + small, bf16),
         ],
         compiler_params=pltpu.CompilerParams(
             collective_id=0, has_side_effects=True, vmem_limit_bytes=60 << 20

time: 99.2 us -> 97.9 us (0.987)
  Pallas kernels: 94.4 us -> 93.1 us
    pallas_call x1, Pallas kernels: 94.4 us -> 93.1 us  [step(): pl.pallas_call(functools.partial(step_kernel, scale), out_shape=(jax.Shap...]
where the time goes in v7:
time: 97.9 us; the launch traced here: 97.8 us
  Pallas kernels  93.1 us (95%)
  other arithmetic  2.55 us (3%)
  between operations  1.29 us (1%)
    pallas_call x1, Pallas kernels, step(): pl.pallas_call(functools.partial(step_kernel, scale), out_shape=(jax.Shap...  93.1 us
    convert_element_type x1, other arithmetic, per_device(): table_grad = table_sum.astype(jnp.float32)  2.55 us

profile of v7, /device:TPU:1, one launch (start us, length us, event | category | flops | bytes accessed | tf_op | source)
XLA Modules:
  0.0 97.8 jit_solution(17478625331114590120)
XLA Ops:
  1.3 93.1 %shard_map.86 = (bf16[768,512]{1,0:T(8,128)(2,1)}, bf16[512,512]{1,0:T(8,128)(2,1)}) custom-call(s32[1]{0:T(128)S(6)} %copy.10.lengths, bf16[768,512]{1,0:T(8,128)(2,1)} %table_far.1, s32[1,256]{1,0:T(1,128)} %bitcast.3, s32[1,256]{1,0:T(1,128)} %rows.1, bf16[512,2048]{1,0:T(8,128)(2,1)} %w_in_far.1, bf16[512,512]{1,0:T(8,128)(2,1)} %w_out_far.1, ...), custom_call_target="tpu_custom_call" | custom-call | tf_op jit(solution)/shard_map/pallas_call | solution.py:634
  94.4 0.0 copy-start
  94.4 2.5 %convert_element_type.3 = f32[768,512]{1,0:T(8,128)} convert(bf16[768,512]{1,0:T(8,128)(2,1)} %get-tuple-element.4) | non-fusion elementwise | flops 393216 | bytes 2359296 | tf_op jit(solution)/shard_map/convert_element_type | solution.py:722
  97.0 0.0 copy-done
  97.0 0.8 copy.11
Async XLA Ops:
  94.4 2.6 %copy-start = (bf16[512,512]{1,0:T(8,128)(2,1)S(1)}, bf16[512,512]{1,0:T(8,128)(2,1)}, u32[]{:S(2)}) copy-start(bf16[512,512]{1,0:T(8,128)(2,1)} %get-tuple-element.9) | copy-start | bytes 1572868

commit v8 on v7

--- a/solution.py
+++ b/solution.py
@@ -91,7 +91,7 @@
     f32, bf16 = jnp.float32, jnp.bfloat16
 
     def zp(k):
-        return lax.rem(me + k, nz)
+        return lax.rem(me + nz // 2 + (k // 2) * (1 - 2 * lax.rem(k, 2)) + nz, nz)
 
     def xp(k):
         return lax.rem(x + k, NX)
@@ -400,7 +400,7 @@
     f32, bf16 = jnp.float32, jnp.bfloat16
 
     def zp(k):
-        return lax.rem(me + k, nz)
+        return lax.rem(me + nz // 2 + (k // 2) * (1 - 2 * lax.rem(k, 2)) + nz, nz)
 
     own = owners[...]
     hits = (lax.broadcasted_iota(jnp.int32, (nz, slots), 0) == own).astype(f32)

time: 97.9 us -> 96 us (0.981)
  Pallas kernels: 93.1 us -> 91.2 us
    pallas_call x1, Pallas kernels: 93.1 us -> 91.2 us  [step(): pl.pallas_call(functools.partial(step_kernel, scale), out_shape=(jax.Shap...]
where the time goes in v8:
time: 96 us; the launch traced here: 95.8 us
  Pallas kernels  91.2 us (95%)
  other arithmetic  2.55 us (3%)
  between operations  1.29 us (1%)
    pallas_call x1, Pallas kernels, step(): pl.pallas_call(functools.partial(step_kernel, scale), out_shape=(jax.Shap...  91.2 us
    convert_element_type x1, other arithmetic, per_device(): table_grad = table_sum.astype(jnp.float32)  2.55 us

profile of v8, /device:TPU:1, one launch (start us, length us, event | category | flops | bytes accessed | tf_op | source)
XLA Modules:
  0.0 95.8 jit_solution(14118727352498373293)
XLA Ops:
  1.3 91.2 %shard_map.86 = (bf16[768,512]{1,0:T(8,128)(2,1)}, bf16[512,512]{1,0:T(8,128)(2,1)}) custom-call(s32[1]{0:T(128)S(6)} %copy.10.lengths, bf16[768,512]{1,0:T(8,128)(2,1)} %table_far.1, s32[1,256]{1,0:T(1,128)} %bitcast.3, s32[1,256]{1,0:T(1,128)} %rows.1, bf16[512,2048]{1,0:T(8,128)(2,1)} %w_in_far.1, bf16[512,512]{1,0:T(8,128)(2,1)} %w_out_far.1, ...), custom_call_target="tpu_custom_call" | custom-call | tf_op jit(solution)/shard_map/pallas_call | solution.py:634
  92.5 0.0 copy-start
  92.5 2.5 %convert_element_type.3 = f32[768,512]{1,0:T(8,128)} convert(bf16[768,512]{1,0:T(8,128)(2,1)} %get-tuple-element.4) | non-fusion elementwise | flops 393216 | bytes 2359296 | tf_op jit(solution)/shard_map/convert_element_type | solution.py:722
  95.0 0.0 copy-done
  95.0 0.8 copy.11
Async XLA Ops:
  92.5 2.6 %copy-start = (bf16[512,512]{1,0:T(8,128)(2,1)S(1)}, bf16[512,512]{1,0:T(8,128)(2,1)}, u32[]{:S(2)}) copy-start(bf16[512,512]{1,0:T(8,128)(2,1)} %get-tuple-element.9) | copy-start | bytes 1572868
